TPU v7x, 32 devices: a whole 2x2x4 slice. The times are simulated.
32 devices in a mesh: dp: 8 (over z, y), tensor: 4 (over x, core).
Axes of the slice: x: 2, y: 2, z: 4, core: 2. Of those that a mesh axis runs over, the one named last changes fastest.
Arguments:
- attn_out: bfloat16 [1280, 2048], P('dp', 'tensor'), may hold values from -6 to 6
- residual: bfloat16 [1280, 2048], P(('dp', 'tensor')), may hold values from -6 to 6
- out_weight: bfloat16 [2048, 2048], P('tensor'), may hold values from -0.125 to 0.125
- norm_gain: float32 [2048], replicated, may hold values from 0.25 to 1.75
- router_weight: bfloat16 [2048, 64], replicated, may hold values from -0.125 to 0.125
- routes: int32 [1280, 8], P(('dp', 'tensor')), may hold values from 0 to 63, all different within a row; in each aligned block of 40 rows (0 to 39, 40 to 79, ...) at most 8 rows name the same one
- gate_up: bfloat16 [64, 2048, 2, 1024], P('dp', None, None, 'tensor'), may hold values from -0.125 to 0.125
- down_weight: bfloat16 [64, 1024, 2048], P('dp', 'tensor'), may hold values from -0.1875 to 0.1875
- final_gain: float32 [2048], replicated, may hold values from 0.25 to 1.75
- kv_pages: bfloat16 [256, 16, 16, 256], P('dp', None, 'tensor'), may hold values from -6 to 6
- page_pick: int32 [8, 2], P('dp'), may hold values from 0 to 31
- destination: int32 [8, 2], P('dp'), may hold values from 0 to 7, as said below
Outputs:
- new_residual: bfloat16 [1280, 2048], P(('dp', 'tensor'))
- normed: bfloat16 [1280, 2048], P(('dp', 'tensor'))
- arrived: bfloat16 [16, 16, 16, 256], P('dp', None, 'tensor')
Inputs may be any that keep to these rules, and one draw needn't show every extreme that they name: `routes`: each row names 8 different experts; within the rows of one device (aligned blocks of 40 rows) no expert is named by more than 8 rows. `destination`: each column is a permutation of the indices of dp.
All inputs are finite; a program needn't handle non-finite values.
Results may differ from a plain program's by a relative error of at most 0.02.
Values may be sent and summed in bfloat16 or wider, within the bound.
A program may use at most 192 MiB of HBM per device.

v0:
```python
import jax
import jax.numpy as jnp
from jax import lax
from jax.sharding import PartitionSpec as P

CAP = 8


def rms_scale(values, gain_vec):
    mean_sq = jnp.mean(values * values, axis=-1, keepdims=True)
    return values * lax.rsqrt(mean_sq + 1e-06) * gain_vec


def per_device(
    attn_out,
    residual,
    out_weight,
    norm_gain,
    router_weight,
    routes,
    gate_up,
    down_weight,
    final_gain,
    kv_pages,
    page_pick,
    destination,
):
    groups = lax.axis_size("dp")
    chosen_pages = kv_pages[page_pick[0]]
    owners = jnp.arange(groups, dtype=jnp.int32)[:, None] == destination[0][None, :]
    outgoing = jnp.where(
        owners[:, :, None, None, None], chosen_pages[None], jnp.zeros((), kv_pages.dtype)
    )
    incoming = lax.all_to_all(outgoing, "dp", split_axis=0, concat_axis=0, tiled=True)
    arrived = jnp.sum(incoming, axis=0)
    tok_rows = residual.shape[0]
    width = residual.shape[1]
    projected = lax.psum_scatter(
        jnp.dot(attn_out, out_weight, preferred_element_type=jnp.float32).astype(jnp.bfloat16),
        "tensor",
        scatter_dimension=0,
        tiled=True,
    ).astype(jnp.float32)
    mixed_sum = residual.astype(jnp.float32) + projected
    normed_in = rms_scale(mixed_sum, norm_gain).astype(jnp.bfloat16)
    logits = jnp.dot(normed_in, router_weight, preferred_element_type=jnp.float32)
    experts = router_weight.shape[1]
    capacity = CAP
    top_count = routes.shape[1]
    onehot = (routes[:, :, None] == jnp.arange(experts, dtype=jnp.int32)[None, None, :]).astype(
        jnp.int32
    )
    flat_hits = onehot.reshape(tok_rows * top_count, experts)
    earlier = jnp.cumsum(flat_hits, axis=0) - flat_hits
    slot_rank = jnp.sum(earlier * flat_hits, axis=1)
    slot_index = routes.reshape(-1) * capacity + slot_rank
    picked = jnp.sum(logits[:, None, :] * onehot.astype(jnp.float32), axis=2)
    gate_values = jax.nn.sigmoid(picked).astype(jnp.bfloat16)
    slot_table = (
        slot_index[:, None] == jnp.arange(experts * capacity, dtype=jnp.int32)[None, :]
    ).reshape(tok_rows, top_count, experts * capacity)
    placement = jnp.any(slot_table, axis=1).astype(jnp.bfloat16)
    send_rows = jnp.einsum(
        "ts,td->sd", placement, normed_in, preferred_element_type=jnp.float32
    ).astype(jnp.bfloat16)
    send_rows = send_rows.reshape(groups, -1, width)
    received = lax.all_to_all(send_rows, "dp", split_axis=0, concat_axis=0, tiled=True)
    local_experts = gate_up.shape[0]
    received = received.reshape(groups, local_experts, capacity, width)
    paired = jnp.einsum(
        "necd,edgf->necgf",
        received,
        lax.all_gather(gate_up, "tensor", axis=3, tiled=True),
        preferred_element_type=jnp.float32,
    )
    hidden = (jax.nn.silu(paired[..., 0, :]) * paired[..., 1, :]).astype(jnp.bfloat16)
    summed = jnp.einsum(
        "necf,efd->necd",
        hidden,
        lax.all_gather(down_weight, "tensor", axis=1, tiled=True),
        preferred_element_type=jnp.float32,
    )
    expert_out = summed.astype(jnp.bfloat16).reshape(groups, -1, width)
    returned = lax.all_to_all(expert_out, "dp", split_axis=0, concat_axis=0, tiled=True).reshape(
        experts * capacity, width
    )
    gate_matrix = jnp.einsum(
        "tks,tk->ts", slot_table.astype(jnp.float32), gate_values.astype(jnp.float32)
    ).astype(jnp.bfloat16)
    moe_sum = jnp.dot(gate_matrix, returned, preferred_element_type=jnp.float32)
    combined = mixed_sum + moe_sum
    new_residual = combined.astype(jnp.bfloat16)
    normed = rms_scale(combined, final_gain).astype(jnp.bfloat16)
    return (new_residual, normed, arrived)


def solution(mesh):
    in_specs = (
        P("dp", "tensor"),
        P(("dp", "tensor"), None),
        P("tensor", None),
        P(),
        P(),
        P(("dp", "tensor"), None),
        P("dp", None, None, "tensor"),
        P("dp", "tensor", None),
        P(),
        P("dp", None, "tensor", None),
        P("dp", None),
        P("dp", None),
    )
    out_specs = (
        P(("dp", "tensor"), None),
        P(("dp", "tensor"), None),
        P("dp", None, "tensor", None),
    )
    return jax.shard_map(
        per_device, mesh=mesh, in_specs=in_specs, out_specs=out_specs, check_vma=False
    )
```

profile of v0, /device:TPU:0, one launch (start us, length us, event | category | flops | bytes accessed | tf_op | source)
XLA Modules:
  0.0 726.2 jit_solution(17687883327890902005)
XLA Ops:
  7.2 0.0 copy-start
  7.2 0.0 reduce-scatter.2.cloned.1.call-start
  7.2 1.5 copy-done
  8.8 2.3 convolution_convert_fusion.1
  11.1 0.0 reduce-scatter.2.cloned.1.call-update
  11.1 0.0 all-gather.3.cloned.1.call-start
  11.1 15.3 %copy.45 = bf16[8,2048,2,256]{3,1,2,0:T(8,128)(2,1)} copy(bf16[8,2048,2,256]{3,2,1,0:T(2,128)(2,1)} %param.18) | data formatting | bytes 33554432 | tf_op args[6]
  26.5 0.0 all-gather.3.cloned.1.call-update
  26.5 0.0 copy-start.6
  26.5 0.0 copy-start.2
  26.5 0.0 copy-start.4
  26.5 0.0 all-gather.5.cloned.1.call-start
  26.6 0.7 all-gather.5.cloned.1.call-update
  27.3 0.1 copy.39
  27.4 0.1 eq.62
  27.5 0.9 reduce-window.6
  28.4 0.2 slice_reduce_fusion
  28.7 0.1 bitcast_bitcast_fusion
  28.8 0.1 reduce_sum.51
  28.9 0.3 fusion.18
  29.2 7.3 %reduce-scatter.2.cloned.1.call-done = bf16[40,2048]{1,0:T(8,128)(2,1)} async-done(((bf16[160,2048]{1,0:T(8,128)(2,1)}), bf16[40,2048]{1,0:T(8,128)(2,1)}) %reduce-scatter.2.cloned.1.call-update) | async-done | bytes 163856 | tf_op jit(solution)/shard_map/reduce_scatter | solution.py:38
  36.5 1.1 multiply_reduce_fusion.1
  37.5 0.0 copy-done.4
  37.5 3.0 convolution_convert_fusion
  40.5 5.7 all-to-all-start
  46.3 2.2 gather_fusion
  48.5 0.9 broadcast_select_fusion
  49.5 45.0 %all-to-all-done = bf16[8,64,2048]{2,1,0:T(8,128)(2,1)S(1)} async-done(((bf16[8,64,2048]{2,1,0:T(8,128)(2,1)}), bf16[8,64,2048]{2,1,0:T(8,128)(2,1)S(1)}, u32[]{:S(2)}, u32[]{:S(2)}) %all-to-all-start) | async-done | bytes 2097184 | tf_op jit(solution)/shard_map/all_to_all | solution.py:67
  94.5 3.6 all-to-all-start.2
  98.1 341.7 %all-gather.3.cloned.1.call-done = bf16[8,2048,2,1024]{3,1,2,0:T(8,128)(2,1)} async-done(((bf16[8,2048,2,256]{3,1,2,0:T(8,128)(2,1)}), bf16[8,2048,2,1024]{3,1,2,0:T(8,128)(2,1)}) %all-gather.3.cloned.1.call-update) | async-done | bytes 67108880 | tf_op jit(solution)/shard_map/all_gather | solution.py:73
  439.8 36.2 %fusion.10 = f32[8,8,8,2,1024]{4,2,3,0,1:T(8,128)} fusion(bf16[8,2048,2,1024]{3,1,2,0:T(8,128)(2,1)} %all-gather.3.cloned.1.call-done, bf16[8,64,2048]{2,1,0:T(8,128)(2,1)S(1)} %all-to-all-done), kind=kOutput, calls=%fused_computation.10 | convolution fusion | flops 4294967296 | bytes 73400320 | tf_op jit(solution)/shard_map/necd,edgf->necgf/dot_general | solution.py:70
  476.0 166.9 %all-gather.5.cloned.1.call-done = bf16[8,1024,2048]{2,1,0:T(8,128)(2,1)} async-done(((bf16[8,256,2048]{2,1,0:T(8,128)(2,1)}), bf16[8,1024,2048]{2,1,0:T(8,128)(2,1)}) %all-gather.5.cloned.1.call-update) | async-done | bytes 33554448 | tf_op jit(solution)/shard_map/all_gather | solution.py:80
  642.9 17.7 %fusion.7 = bf16[8,8,8,2048]{3,2,0,1:T(8,128)(2,1)S(1)} fusion(bf16[8,1024,2048]{2,1,0:T(8,128)(2,1)} %all-gather.5.cloned.1.call-done, f32[8,8,8,2,1024]{4,2,3,0,1:T(8,128)} %fusion.10), kind=kOutput, calls=%fused_computation.7 | convolution fusion | flops 2151677952 | bytes 39845888 | tf_op jit(solution)/shard_map/necf,efd->necd/dot_general | solution.py:77
  660.7 1.6 copy.70
  662.3 0.0 all-to-all-done.2
  662.3 5.6 all-to-all-start.1
  667.9 0.1 reduce_sum.55
  668.0 0.0 copy-start.5
  668.0 0.7 copy.50
  668.7 0.3 fusion.26
  668.9 0.2 multiply_reduce_fusion.2
  669.2 0.1 copy.44
  669.2 0.1 copy.51
  669.3 0.3 fusion.19
  669.7 47.0 %all-to-all-done.1 = bf16[8,64,2048]{2,1,0:T(8,128)(2,1)} async-done(((bf16[8,64,2048]{2,1,0:T(8,128)(2,1)}), bf16[8,64,2048]{2,1,0:T(8,128)(2,1)}, u32[]{:S(2)}, u32[]{:S(2)}) %all-to-all-start.1) | async-done | bytes 2097184 | tf_op jit(solution)/shard_map/all_to_all | solution.py:84
  716.7 2.2 multiply_reduce_fusion
  718.9 0.0 copy-done.5
  718.9 0.8 multiply_convert_fusion
  (24 shorter events, 0.2 us)
Async XLA Ops:
  7.2 1.6 copy-start
  7.2 29.3 %reduce-scatter.2.cloned.1.call-start = ((), (), s32[]{:S(2)}) async-start(), calls=%async_computation.4 | async-start | bytes 819200 | tf_op jit(solution)/shard_map/reduce_scatter | solution.py:38
  11.1 428.7 %all-gather.3.cloned.1.call-start = ((), (), s32[]{:S(2)}) async-start(), calls=%async_computation.5 | async-start | bytes 83886080 | tf_op jit(solution)/shard_map/all_gather | solution.py:73
  26.5 0.8 copy-start.6
  26.5 9.9 %copy-start.2 = (bf16[40,2048]{1,0:T(8,128)(2,1)S(1)}, bf16[40,2048]{1,0:T(8,128)(2,1)}, u32[]{:S(2)}) copy-start(bf16[40,2048]{1,0:T(8,128)(2,1)} %param.13) | copy-start | bytes 491524
  26.5 11.0 %copy-start.4 = (f32[2048]{0:T(1024)S(1)}, f32[2048]{0:T(1024)}, u32[]{:S(2)}) copy-start(f32[2048]{0:T(1024)} %param.15) | copy-start | bytes 24580
  26.5 616.4 %all-gather.5.cloned.1.call-start = ((), (), s32[]{:S(2)}) async-start(), calls=%async_computation.6 | async-start | bytes 41943040 | tf_op jit(solution)/shard_map/all_gather | solution.py:80
  40.5 5.7 copy-start.8
  40.5 8.0 %copy-start.9 = (s32[1,2]{1,0:T(1,128)S(1)}, s32[1,2]{1,0:T(1,128)}, u32[]{:S(2)}) copy-start(s32[1,2]{1,0:T(1,128)} %param.23) | copy-start | bytes 28
  40.5 53.9 %all-to-all-start = ((bf16[8,64,2048]{2,1,0:T(8,128)(2,1)}), bf16[8,64,2048]{2,1,0:T(8,128)(2,1)S(1)}, u32[]{:S(2)}, u32[]{:S(2)}) async-start(bf16[8,64,2048]{2,1,0:T(8,128)(2,1)} %bitcast.3), calls=%async_computation.1 | async-start | bytes 4194304 | tf_op jit(solution)/shard_map/all_to_all | solution.py:67
  94.5 567.8 %all-to-all-start.2 = ((bf16[8,2,16,4,256]{4,2,3,1,0:T(8,128)(2,1)}), bf16[8,2,16,4,256]{4,2,3,1,0:T(8,128)(2,1)S(1)}, u32[]{:S(2)}, u32[]{:S(2)}) async-start(bf16[8,2,16,4,256]{4,2,3,1,0:T(8,128)(2,1)} %broadcast_select_fusion), calls=%async_computation.3 | async-start | bytes 1048576 | tf_op jit(solution)/shard_map/all_to_all | solution.py:34
  662.3 6.4 copy-start.3
  662.3 6.4 copy-start.7
  662.3 54.4 %all-to-all-start.1 = ((bf16[8,64,2048]{2,1,0:T(8,128)(2,1)}), bf16[8,64,2048]{2,1,0:T(8,128)(2,1)}, u32[]{:S(2)}, u32[]{:S(2)}) async-start(bf16[8,64,2048]{2,1,0:T(8,128)(2,1)} %bitcast.76), calls=%async_computation.2 | async-start | bytes 4194304 | tf_op jit(solution)/shard_map/all_to_all | solution.py:84
  668.0 50.9 %copy-start.5 = (f32[2048]{0:T(1024)S(1)}, f32[2048]{0:T(1024)}, u32[]{:S(2)}) copy-start(f32[2048]{0:T(1024)} %param.20) | copy-start | bytes 24580
  668.7 51.0 %copy-start.1 = (bf16[512,2048]{1,0:T(8,128)(2,1)S(1)}, bf16[512,2048]{1,0:T(8,128)(2,1)}, u32[]{:S(2)}) copy-start(bf16[512,2048]{1,0:T(8,128)(2,1)} %param.14) | copy-start | bytes 6291460
Sparse Core Ops, SparseCore 0:
  11.2 25.2 reduce-scatter.1
  38.0 401.7 all-gather.2
  441.4 201.5 all-gather.4
where the time goes:
time: 727 us; the launch traced here: 726 us
  waiting for transfers between devices  609 us (84%)
  matrix products  61.9 us (9%)
  local copies, waits for them, and re-layouts  22.1 us (3%)
  starting transfers between devices  15.1 us (2%)
  between operations  14 us (2%)
    all_gather x1, waiting for transfers between devices, per_device(): lax.all_gather(gate_up, 'tensor', axis=3, tiled=True)  342 us
    all_gather x1, waiting for transfers between devices, per_device(): lax.all_gather(down_weight, 'tensor', axis=1, tiled=True)  167 us
    all_to_all x1, waiting for transfers between devices, per_device(): lax.all_to_all(expert_out, 'dp', split_axis=0, concat_axis=0, tiled=True)  47 us
    all_to_all x1, waiting for transfers between devices, per_device(): lax.all_to_all(send_rows, 'dp', split_axis=0, concat_axis=0, tiled=True)  45 us
    dot_general x1, matrix products, per_device(): jnp.einsum('necd,edgf->necgf', received, lax.all_gather(gate_up, 'tensor'...  36.2 us
    dot_general x1, matrix products, per_device(): jnp.einsum('necf,efd->necd', hidden, lax.all_gather(down_weight, 'tensor'...  17.7 us
    unnamed x23, local copies, waits for them, and re-layouts  17.7 us
  transfers between devices with their start and end apart: 6, of which 5 were waited for; matrix products, arithmetic and copies ran while one was open for 11% of the time, Pallas kernels for 0%

commit v1 on v0

v1 whole, which is shorter than its diff:
```python
import jax
import jax.numpy as jnp
from jax import lax
from jax.sharding import PartitionSpec as P

CAP = 8


def rms_scale(values, gain_vec):
    mean_sq = jnp.mean(values * values, axis=-1, keepdims=True)
    return values * lax.rsqrt(mean_sq + 1e-06) * gain_vec


def migrate(kv_pages, page_pick, destination):
    groups = lax.axis_size("dp")
    chosen_pages = kv_pages[page_pick[0]]
    owners = jnp.arange(groups, dtype=jnp.int32)[:, None] == destination[0][None, :]
    outgoing = jnp.where(
        owners[:, :, None, None, None], chosen_pages[None], jnp.zeros((), kv_pages.dtype)
    )
    incoming = lax.all_to_all(outgoing, "dp", split_axis=0, concat_axis=0, tiled=True)
    return jnp.sum(incoming, axis=0)


def local_slots(routes_all, first, local_experts, groups, shards, rows):
    hits = jnp.any(
        routes_all[:, :, None] == first + jnp.arange(local_experts, dtype=jnp.int32), axis=1
    )
    hits = hits.reshape(groups, shards * rows, local_experts)
    token = jnp.arange(shards * rows, dtype=jnp.int32)
    before = (token[:, None] > token[None, :]) & (
        token[:, None] // rows == token[None, :] // rows
    )
    rank = jnp.einsum(
        "ut,bte->bue",
        before.astype(jnp.bfloat16),
        hits.astype(jnp.bfloat16),
        preferred_element_type=jnp.float32,
    ).astype(jnp.int32)
    within = (token // rows * CAP)[None, :, None] + rank
    within = jnp.where(hits, within, -1)
    slots = jnp.arange(shards * CAP, dtype=jnp.int32)
    table = within[:, :, :, None] == slots
    return table.reshape(groups, shards * rows, local_experts * shards * CAP)


def per_device(
    attn_out,
    residual,
    out_weight,
    norm_gain,
    router_weight,
    routes,
    gate_up,
    down_weight,
    final_gain,
    kv_pages,
    page_pick,
    destination,
):
    groups = lax.axis_size("dp")
    shards = lax.axis_size("tensor")
    rows, width = residual.shape
    local_experts = gate_up.shape[0]
    first = lax.axis_index("dp") * local_experts
    arrived = migrate(kv_pages, page_pick, destination)
    routes_all = lax.all_gather(routes, ("dp", "tensor"), axis=0, tiled=True)
    table = local_slots(routes_all, first, local_experts, groups, shards, rows)
    projected = lax.psum_scatter(
        jnp.dot(attn_out, out_weight, preferred_element_type=jnp.float32).astype(jnp.bfloat16),
        "tensor",
        scatter_dimension=0,
        tiled=True,
    ).astype(jnp.float32)
    mixed_sum = residual.astype(jnp.float32) + projected
    normed_in = rms_scale(mixed_sum, norm_gain).astype(jnp.bfloat16)
    tokens = lax.all_gather(normed_in, ("dp", "tensor"), axis=0, tiled=True)
    local_router = lax.dynamic_slice_in_dim(router_weight, first, local_experts, axis=1)
    logits = jnp.dot(tokens, local_router, preferred_element_type=jnp.float32)
    gates = jax.nn.sigmoid(logits).astype(jnp.bfloat16)
    tokens = tokens.reshape(groups, shards * rows, width)
    gates = jnp.repeat(
        gates.reshape(groups, shards * rows, local_experts), shards * CAP, axis=2
    )
    placement = table.astype(jnp.bfloat16)
    combine = jnp.where(table, gates, jnp.zeros((), jnp.bfloat16))
    slotted = jnp.einsum(
        "bts,btd->bsd", placement, tokens, preferred_element_type=jnp.float32
    ).astype(jnp.bfloat16)
    slotted = slotted.reshape(groups, local_experts, shards * CAP, width)
    paired = jnp.einsum(
        "becd,edgf->becgf", slotted, gate_up, preferred_element_type=jnp.float32
    )
    hidden = (jax.nn.silu(paired[..., 0, :]) * paired[..., 1, :]).astype(jnp.bfloat16)
    expert_out = jnp.einsum(
        "becf,efd->becd", hidden, down_weight, preferred_element_type=jnp.float32
    ).astype(jnp.bfloat16)
    expert_out = expert_out.reshape(groups, local_experts * shards * CAP, width)
    partial = jnp.einsum(
        "bts,bsd->btd", combine, expert_out, preferred_element_type=jnp.float32
    ).astype(jnp.bfloat16)
    moe_sum = lax.psum_scatter(
        partial.reshape(groups * shards * rows, width),
        ("dp", "tensor"),
        scatter_dimension=0,
        tiled=True,
    ).astype(jnp.float32)
    combined = mixed_sum + moe_sum
    new_residual = combined.astype(jnp.bfloat16)
    normed = rms_scale(combined, final_gain).astype(jnp.bfloat16)
    return (new_residual, normed, arrived)


def solution(mesh):
    in_specs = (
        P("dp", "tensor"),
        P(("dp", "tensor"), None),
        P("tensor", None),
        P(),
        P(),
        P(("dp", "tensor"), None),
        P("dp", None, None, "tensor"),
        P("dp", "tensor", None),
        P(),
        P("dp", None, "tensor", None),
        P("dp", None),
        P("dp", None),
    )
    out_specs = (
        P(("dp", "tensor"), None),
        P(("dp", "tensor"), None),
        P("dp", None, "tensor", None),
    )
    return jax.shard_map(
        per_device, mesh=mesh, in_specs=in_specs, out_specs=out_specs, check_vma=False
    )
```

time: 727 us -> 312 us (0.43)
  waiting for transfers between devices: 609 us -> 167 us
  blocking collectives: 0 us -> 62.8 us
  matrix products: 61.9 us -> 46.8 us
  starting transfers between devices: 15.1 us -> 0.12 us
  local copies, waits for them, and re-layouts: 22.1 us -> 13.4 us
    all_gather x2 -> x1, waiting for transfers between devices: 509 us -> 23.4 us  [per_device(): tokens = lax.all_gather(normed_in, ('dp', 'tensor'), axis=0, tiled=True)]
    reduce_scatter x0 -> x1, waiting for transfers between devices: none -> 119 us  [per_device(): lax.psum_scatter(partial.reshape(groups * shards * rows, width), ('dp', '...]
    all_to_all x3 -> x0, waiting for transfers between devices: 92.1 us -> none  [the longest x1 47 us: per_device(): lax.all_to_all(expert_out, 'dp', split_axis=0, concat_axis=0, tiled=True)]
    all_gather x0 -> x1, blocking collectives: none -> 41.5 us  [per_device(): routes_all = lax.all_gather(routes, ('dp', 'tensor'), axis=0, tiled=True)]
    all_to_all x0 -> x1, blocking collectives: none -> 21.3 us  [migrate(): lax.all_to_all(outgoing, 'dp', split_axis=0, concat_axis=0, tiled=True)]
    reduce_scatter x1, waiting for transfers between devices: 7.27 us -> 25.3 us  [per_device(): lax.psum_scatter(jnp.dot(attn_out, out_weight, preferred_element_type=jnp...]
    dot_general x6, matrix products: 59.6 us -> 44.5 us  [the longest x1 14.6 us: per_device(): jnp.einsum('becd,edgf->becgf', slotted, gate_up, preferred_element_type=j...]
    all_to_all x3 -> x0, starting transfers between devices: 15 us -> none  [the longest x1 5.68 us: per_device(): lax.all_to_all(send_rows, 'dp', split_axis=0, concat_axis=0, tiled=True)]
  transfers between devices with their start and end apart: 6 -> 3, of which waited for: 5 -> 3; matrix products, arithmetic and copies ran while one was open for 11% -> 1% of each run, Pallas kernels for 0% -> 0%
where the time goes in v1:
time: 312 us; the launch traced here: 311 us
  waiting for transfers between devices  167 us (54%)
  blocking collectives  62.8 us (20%)
  matrix products  46.8 us (15%)
  between operations  13.9 us (4%)
  local copies, waits for them, and re-layouts  13.4 us (4%)
  other arithmetic  6.75 us (2%)
    reduce_scatter x1, waiting for transfers between devices, per_device(): lax.psum_scatter(partial.reshape(groups * shards * rows, width), ('dp', '...  119 us
    all_gather x1, blocking collectives, per_device(): routes_all = lax.all_gather(routes, ('dp', 'tensor'), axis=0, tiled=True)  41.5 us
    reduce_scatter x1, waiting for transfers between devices, per_device(): lax.psum_scatter(jnp.dot(attn_out, out_weight, preferred_element_type=jnp...  25.3 us
    all_gather x1, waiting for transfers between devices, per_device(): tokens = lax.all_gather(normed_in, ('dp', 'tensor'), axis=0, tiled=True)  23.4 us
    all_to_all x1, blocking collectives, migrate(): lax.all_to_all(outgoing, 'dp', split_axis=0, concat_axis=0, tiled=True)  21.3 us
    dot_general x1, matrix products, per_device(): jnp.einsum('becd,edgf->becgf', slotted, gate_up, preferred_element_type=j...  14.6 us
    dot_general x1, matrix products, per_device(): jnp.einsum('becf,efd->becd', hidden, down_weight, preferred_element_type=...  10.3 us
    convert_element_type x1, local copies, waits for them, and re-layouts, per_device(): expert_out = jnp.einsum('becf,efd->becd', hidden, down_weight, preferred_...  8.25 us
  transfers between devices with their start and end apart: 3, of which 3 were waited for; matrix products, arithmetic and copies ran while one was open for 1% of the time, Pallas kernels for 0%

profile of v1, /device:TPU:0, one launch (start us, length us, event | category | flops | bytes accessed | tf_op | source)
XLA Modules:
  0.0 311.2 jit_solution(3009542011490433842)
XLA Ops:
  7.2 0.0 copy-start
  7.2 0.0 reduce-scatter.3.cloned.1.call-start
  7.2 1.5 copy-done
  8.8 2.3 convolution_convert_fusion.2
  11.0 0.0 reduce-scatter.3.cloned.1.call-update
  11.1 0.0 all-gather.3.cloned.1.call-start
  11.1 25.3 %reduce-scatter.3.cloned.1.call-done = bf16[40,2048]{1,0:T(8,128)(2,1)} async-done(((bf16[160,2048]{1,0:T(8,128)(2,1)}), bf16[40,2048]{1,0:T(8,128)(2,1)}) %reduce-scatter.3.cloned.1.call-update) | async-done | bytes 163856 | tf_op jit(solution)/shard_map/reduce_scatter | solution.py:69
  36.4 1.2 multiply_reduce_fusion.1
  37.5 1.8 multiply_convert_fusion.1
  39.3 0.0 all-gather.3.cloned.1.call-update
  39.3 0.0 reduce-scatter.5.cloned.1.call-start
  39.4 41.5 %all-gather = s32[32,40,8]{1,2,0:T(8,128)S(1)} all-gather(s32[1,40,8]{1,2,0:T(8,128)} %bitcast.68), channel_id=1, replica_groups=mesh['dp'=8,'tensor'=4] {'dp','tensor'}, dimensions={0}, use_global_device_ids=true | all-gather | bytes 42240 | tf_op jit(solution)/shard_map/all_gather | solution.py:67
  80.9 0.1 reshape.179
  81.0 0.1 compare_reduce_fusion
  81.1 0.1 reshape.163
  81.3 0.1 eq.74
  81.3 0.2 fusion.20
  81.6 0.4 bitcast_compare_fusion
  82.0 23.4 %all-gather.3.cloned.1.call-done = bf16[1280,2048]{1,0:T(8,128)(2,1)} async-done(((bf16[40,2048]{1,0:T(8,128)(2,1)}), bf16[1280,2048]{1,0:T(8,128)(2,1)}) %all-gather.3.cloned.1.call-update) | async-done | bytes 5242896 | tf_op jit(solution)/shard_map/all_gather | solution.py:77
  105.3 4.0 %fusion.10 = bf16[1280,8]{0,1:T(8,128)(2,1)S(1)} fusion(bf16[1280,2048]{1,0:T(8,128)(2,1)} %all-gather.3.cloned.1.call-done, bf16[2048,64]{0,1:T(8,128)(2,1)} %param.16, s32[]{:T(128)S(6)} %select_n.54), kind=kOutput, calls=%fused_computation.14 | convolution fusion | flops 41984000 | bytes 5296132 | tf_op jit(solution)/shard_map/dot_general | solution.py:79
  109.3 0.1 reshape.164
  109.4 0.3 bitcast_select_fusion
  109.8 8.0 %convolution_convert_fusion = bf16[8,256,2048]{2,1,0:T(8,128)(2,1)} fusion(pred[8,160,256]{1,2,0:T(32,128)(4,1)S(1)} %bitcast_compare_fusion, bf16[8,160,2048]{2,1,0:T(8,128)(2,1)} %bitcast.65), kind=kOutput, calls=%fused_computation.7 | convolution fusion | flops 1346371584 | bytes 13959168 | tf_op jit(solution)/shard_map/bts,btd->bsd/dot_general | solution.py:87
  117.8 14.6 %fusion.11 = f32[8,8,32,2,256]{4,2,3,0,1:T(8,128)} fusion(bf16[8,2048,2,256,1]{3,2,1,0,4:T(2,128)(2,1)} %bitcast.69, bf16[8,8,32,2048,1]{3,2,1,0,4:T(8,128)(2,1)} %bitcast.67), kind=kOutput, calls=%fused_computation.15 | convolution fusion | flops 4294967296 | bytes 29360128 | tf_op jit(solution)/shard_map/becd,edgf->becgf/dot_general | solution.py:91
  132.4 10.3 %convert_bitcast_fusion = bf16[8,8,32,2048]{3,2,0,1:T(8,128)(2,1)} fusion(bf16[8,256,2048]{2,1,0:T(8,128)(2,1)} %param.19, f32[8,8,32,2,256]{4,2,3,0,1:T(8,128)} %fusion.11), kind=kOutput, calls=%fused_computation.6 | convolution fusion | flops 2154823680 | bytes 20971520 | tf_op jit(solution)/shard_map/becf,efd->becd/dot_general | solution.py:95
  142.7 8.3 %copy.50 = bf16[8,8,32,2048]{3,2,1,0:T(8,128)(2,1)} copy(bf16[8,8,32,2048]{3,2,0,1:T(8,128)(2,1)} %convert_bitcast_fusion) | data formatting | bytes 16777216 | tf_op jit(solution)/shard_map/convert_element_type | solution.py:97
  150.9 0.0 copy-start.1
  150.9 7.4 %convolution_convert_fusion.1 = bf16[8,160,2048]{2,1,0:T(8,128)(2,1)} fusion(bf16[8,160,256]{1,2,0:T(8,128)(2,1)S(1)} %bitcast_select_fusion, bf16[8,256,2048]{2,1,0:T(8,128)(2,1)} %bitcast.64), kind=kOutput, calls=%fused_computation.8 | convolution fusion | flops 1344798720 | bytes 14286848 | tf_op jit(solution)/shard_map/bts,bsd->btd/dot_general | solution.py:99
  158.4 0.0 copy-start.5
  158.4 0.0 copy-start.6
  158.4 0.0 copy-start.2
  158.4 0.0 copy-start.3
  158.4 0.0 copy-start.4
  158.4 0.0 reduce-scatter.5.cloned.1.call-update
  158.4 0.6 copy-done.5
  159.0 1.8 gather_fusion
  160.9 0.0 copy-done.6
  160.9 0.1 broadcast_select_fusion
  161.0 21.3 %all_to_all.5 = bf16[8,2,16,4,256]{4,2,3,1,0:T(8,128)(2,1)S(1)} all-to-all(bf16[8,2,16,4,256]{4,2,3,1,0:T(8,128)(2,1)S(1)} %broadcast_select_fusion), channel_id=1, replica_groups=mesh['dp'=8,'tensor'=4] {'dp'}, dimensions={0} | all-to-all | bytes 1048576 | tf_op jit(solution)/shard_map/all_to_all | solution.py:21
  182.3 0.1 reduce_sum.32
  182.4 0.7 copy.53
  183.1 118.7 %reduce-scatter.5.cloned.1.call-done = bf16[40,2048]{1,0:T(8,128)(2,1)} async-done(((bf16[1280,2048]{1,0:T(8,128)(2,1)}), bf16[40,2048]{1,0:T(8,128)(2,1)}) %reduce-scatter.5.cloned.1.call-update) | async-done | bytes 163856 | tf_op jit(solution)/shard_map/reduce_scatter | solution.py:102
  301.8 0.0 copy-done.2
  301.8 0.0 copy-done.3
  301.8 1.1 multiply_reduce_fusion
  302.9 0.0 copy-done.4
  302.9 1.7 multiply_convert_fusion
  304.6 0.0 copy-done.1
  (11 shorter events, 0.1 us)
Async XLA Ops:
  7.2 1.6 copy-start
  7.2 29.2 %reduce-scatter.3.cloned.1.call-start = ((), (), s32[]{:S(2)}) async-start(), calls=%async_computation.3 | async-start | bytes 819200 | tf_op jit(solution)/shard_map/reduce_scatter | solution.py:69
  11.1 94.3 %all-gather.3.cloned.1.call-start = ((), (), s32[]{:S(2)}) async-start(), calls=%async_computation.4 | async-start | bytes 5406720 | tf_op jit(solution)/shard_map/all_gather | solution.py:77
  39.3 262.5 %reduce-scatter.5.cloned.1.call-start = ((), (), s32[]{:S(2)}) async-start(), calls=%async_computation.5 | async-start | bytes 5406720 | tf_op jit(solution)/shard_map/reduce_scatter | solution.py:102
  150.9 153.7 %copy-start.1 = (bf16[512,2048]{1,0:T(8,128)(2,1)S(1)}, bf16[512,2048]{1,0:T(8,128)(2,1)}, u32[]{:S(2)}) copy-start(bf16[512,2048]{1,0:T(8,128)(2,1)} %param.14) | copy-start | bytes 6291460
  158.4 0.7 copy-start.5
  158.4 2.5 copy-start.6
  158.4 143.4 %copy-start.2 = (bf16[40,2048]{1,0:T(8,128)(2,1)S(1)}, bf16[40,2048]{1,0:T(8,128)(2,1)}, u32[]{:S(2)}) copy-start(bf16[40,2048]{1,0:T(8,128)(2,1)} %param.13) | copy-start | bytes 491524
  158.4 143.4 %copy-start.3 = (bf16[40,2048]{1,0:T(8,128)(2,1)S(1)}, bf16[40,2048]{1,0:T(8,128)(2,1)}, u32[]{:S(2)}) copy-start(bf16[40,2048]{1,0:T(8,128)(2,1)} %reduce-scatter.3.cloned.1.call-done) | copy-start | bytes 491524
  158.4 144.5 %copy-start.4 = (f32[2048]{0:T(1024)S(1)}, f32[2048]{0:T(1024)}, u32[]{:S(2)}) copy-start(f32[2048]{0:T(1024)} %param.20) | copy-start | bytes 24580
Sparse Core Ops, SparseCore 0:
  11.2 25.1 reduce-scatter.2
  39.8 65.4 all-gather.2
  158.5 143.2 reduce-scatter.4

commit v2 on v1

--- a/solution.py
+++ b/solution.py
@@ -1,6 +1,8 @@
 import jax
 import jax.numpy as jnp
 from jax import lax
+from jax.experimental import pallas as pl
+from jax.experimental.pallas import tpu as pltpu
 from jax.sharding import PartitionSpec as P
 
 CAP = 8
@@ -9,6 +11,280 @@
 def rms_scale(values, gain_vec):
     mean_sq = jnp.mean(values * values, axis=-1, keepdims=True)
     return values * lax.rsqrt(mean_sq + 1e-06) * gain_vec
+
+
+MESH = pl.DeviceIdType.MESH
+EXTRA = 128
+
+
+class Place:
+    def __init__(self):
+        group, shard = lax.axis_index("dp"), lax.axis_index("tensor")
+        self.z, self.y = group // 2, group % 2
+        self.x, self.c = shard // 2, shard % 2
+        self.core_peer = (group, self.x * 2 + 1 - self.c)
+        self.x_peer = (group, (1 - self.x) * 2 + self.c)
+        self.y_peer = (self.z * 2 + 1 - self.y, shard)
+        self.z_peers = [None] + [(((self.z + j) % 4) * 2 + self.y, shard) for j in (1, 2, 3)]
+
+    def enter(self):
+        barrier = pltpu.get_barrier_semaphore()
+        peers = [self.core_peer, self.x_peer, self.y_peer] + self.z_peers[1:]
+        for peer in peers:
+            pl.semaphore_signal(barrier, inc=1, device_id=peer, device_id_type=MESH)
+        pl.semaphore_wait(barrier, len(peers))
+
+
+def sender(send_sems, recv_sems):
+    used = []
+
+    def send(source, target, peer):
+        index = len(used)
+        copy = pltpu.make_async_remote_copy(
+            src_ref=source,
+            dst_ref=target,
+            send_sem=send_sems.at[index],
+            recv_sem=recv_sems.at[index],
+            device_id=peer,
+            device_id_type=MESH,
+        )
+        copy.start()
+        used.append(copy)
+        return copy
+
+    return send, used
+
+
+def front_kernel(
+    attn_ref, weight_ref, residual_ref, gain_ref, extra_ref, mixed_ref, all_ref,
+    made, core_in, x_out, x_in, own, own_sem, send_sems, recv_sems,
+):
+    at = Place()
+    z, y, x, c = at.z, at.y, at.x, at.c
+    at.enter()
+    send, used = sender(send_sems, recv_sems)
+    rows, width = residual_ref.shape
+    step = 512
+    for start in range(0, width, step):
+        part = jnp.dot(
+            attn_ref[...], weight_ref[:, start : start + step], preferred_element_type=jnp.float32
+        )
+        for shard in range(4):
+            made[shard, :, start : start + step] = part[
+                shard * rows : (shard + 1) * rows
+            ].astype(jnp.bfloat16)
+    to_core_far = send(made.at[(1 - x) * 2 + 1 - c], core_in.at[0], at.core_peer)
+    to_core_near = send(made.at[x * 2 + 1 - c], core_in.at[1], at.core_peer)
+    to_core_far.wait_recv()
+    x_out[...] = (
+        made[(1 - x) * 2 + c].astype(jnp.float32) + core_in[0].astype(jnp.float32)
+    ).astype(jnp.bfloat16)
+    to_x = send(x_out, x_in, at.x_peer)
+    to_core_near.wait_recv()
+    mixed = (
+        residual_ref[...].astype(jnp.float32)
+        + made[x * 2 + c].astype(jnp.float32)
+        + core_in[1].astype(jnp.float32)
+    )
+    to_x.wait_recv()
+    mixed = mixed + x_in[...].astype(jnp.float32)
+    mixed_ref[...] = mixed
+    mean_sq = jnp.mean(mixed * mixed, axis=-1, keepdims=True)
+    own[:, :width] = (mixed * lax.rsqrt(mean_sq + 1e-06) * gain_ref[...]).astype(jnp.bfloat16)
+    own[:, width:] = extra_ref[...]
+
+    half = width // 2
+    columns = [pl.ds(0, half), pl.ds(half, half + EXTRA)]
+    first_peer, second_peer = [at.y_peer, at.x_peer], [at.x_peer, at.y_peer]
+
+    def block(h, zs, first_other, second_other):
+        ys = first_other if h == 0 else second_other
+        xs = second_other if h == 0 else first_other
+        return all_ref.at[zs, 1 - y if ys else y, 1 - x if xs else x, c, :, columns[h]]
+
+    def source(j):
+        return (z + 4 - j) % 4
+
+    z_copies, first_copies, second_copies, core_copies = {}, {}, {}, []
+    for j in (1, 2, 3):
+        for h in (0, 1):
+            z_copies[h, j] = send(own.at[:, columns[h]], block(h, z, 0, 0), at.z_peers[j])
+    keep = pltpu.make_async_copy(own, all_ref.at[z, y, x, c], own_sem)
+    keep.start()
+    for j in range(4):
+        for h in (0, 1):
+            mine = block(h, source(j), 0, 0)
+            if j:
+                z_copies[h, j].wait_recv()
+            held = mine if j else own.at[:, columns[h]]
+            first_copies[h, j] = send(held, mine, first_peer[h])
+            second_copies[h, j, 0] = send(held, mine, second_peer[h])
+            core_copies.append(send(held, mine, at.core_peer))
+    for j in range(4):
+        for h in (0, 1):
+            first_copies[h, j].wait_recv()
+            mine = block(h, source(j), 1, 0)
+            second_copies[h, j, 1] = send(mine, mine, second_peer[h])
+            core_copies.append(send(mine, mine, at.core_peer))
+    for other in (0, 1):
+        for j in range(4):
+            for h in (0, 1):
+                second_copies[h, j, other].wait_recv()
+                mine = block(h, source(j), other, 1)
+                core_copies.append(send(mine, mine, at.core_peer))
+    for copy in core_copies:
+        copy.wait_recv()
+    for copy in used:
+        copy.wait_send()
+    keep.wait()
+
+
+FRONT_COPIES = 3 + 2 * (3 + 4 + 8 + 16)
+
+
+def front(attn_out, out_weight, residual, norm_gain, extra):
+    rows, width = residual.shape
+    vmem = pl.BlockSpec(memory_space=pltpu.VMEM)
+    return pl.pallas_call(
+        front_kernel,
+        out_shape=(
+            jax.ShapeDtypeStruct((rows, width), jnp.float32),
+            jax.ShapeDtypeStruct((4, 2, 2, 2, rows, width + EXTRA), jnp.bfloat16),
+        ),
+        in_specs=[vmem] * 5,
+        out_specs=(vmem, pl.BlockSpec(memory_space=pl.ANY)),
+        scratch_shapes=[
+            pltpu.VMEM((4, rows, width), jnp.bfloat16),
+            pltpu.VMEM((2, rows, width), jnp.bfloat16),
+            pltpu.VMEM((rows, width), jnp.bfloat16),
+            pltpu.VMEM((rows, width), jnp.bfloat16),
+            pltpu.VMEM((rows, width + EXTRA), jnp.bfloat16),
+            pltpu.SemaphoreType.DMA,
+            pltpu.SemaphoreType.DMA((FRONT_COPIES,)),
+            pltpu.SemaphoreType.DMA((FRONT_COPIES,)),
+        ],
+        compiler_params=pltpu.CompilerParams(
+            collective_id=0, has_side_effects=True, vmem_limit_bytes=40 << 20
+        ),
+        name="front",
+    )(attn_out, out_weight, residual, norm_gain.reshape(1, width), extra)
+
+
+def back_kernel(
+    partial_ref, mixed_ref, gain_ref, new_ref, normed_ref,
+    core_in, first_out, first_in, second_out, second_in, z_out, z_in, send_sems, recv_sems,
+):
+    at = Place()
+    z, y, x, c = at.z, at.y, at.x, at.c
+    at.enter()
+    send, used = sender(send_sems, recv_sems)
+    rows, width = mixed_ref.shape
+    half = width // 2
+    columns = [pl.ds(0, half), pl.ds(half, half)]
+    first_peer, second_peer = [at.x_peer, at.y_peer], [at.y_peer, at.x_peer]
+    order = (1, 2, 3, 0)
+
+    def block(h, j, first_other, second_other, core):
+        xs = first_other if h == 0 else second_other
+        ys = second_other if h == 0 else first_other
+        return (
+            (z + j) % 4, 1 - y if ys else y, 1 - x if xs else x, core, slice(None), columns[h],
+        )
+
+    def wide(value):
+        return value.astype(jnp.float32)
+
+    core_copies, first_copies, second_copies, z_copies = {}, {}, {}, {}
+    for first_other in (1, 0):
+        for j in order:
+            for h in (0, 1):
+                for second_other in (1, 0):
+                    slot = (h, first_other, j, second_other)
+                    core_copies[slot] = send(
+                        partial_ref.at[block(h, j, first_other, second_other, 1 - c)],
+                        core_in.at[slot],
+                        at.core_peer,
+                    )
+    for j in order:
+        for h in (0, 1):
+            for second_other in (1, 0):
+                core_copies[h, 1, j, second_other].wait_recv()
+                first_out[h, j, second_other] = (
+                    wide(partial_ref[block(h, j, 1, second_other, c)])
+                    + wide(core_in[h, 1, j, second_other])
+                ).astype(jnp.bfloat16)
+                slot = (h, j, second_other)
+                first_copies[slot] = send(first_out.at[slot], first_in.at[slot], first_peer[h])
+
+    def gathered(h, j, second_other):
+        core_copies[h, 0, j, second_other].wait_recv()
+        first_copies[h, j, second_other].wait_recv()
+        return (
+            wide(partial_ref[block(h, j, 0, second_other, c)])
+            + wide(core_in[h, 0, j, second_other])
+            + wide(first_in[h, j, second_other])
+        )
+
+    for j in order:
+        for h in (0, 1):
+            second_out[h, j] = gathered(h, j, 1).astype(jnp.bfloat16)
+            second_copies[h, j] = send(second_out.at[h, j], second_in.at[h, j], second_peer[h])
+    for j in order:
+        for h in (0, 1):
+            total = gathered(h, j, 0)
+            second_copies[h, j].wait_recv()
+            total = total + wide(second_in[h, j])
+            if j:
+                z_out[h, j - 1] = total.astype(jnp.bfloat16)
+                z_copies[h, j] = send(z_out.at[h, j - 1], z_in.at[h, j - 1], at.z_peers[j])
+            else:
+                mixed_half = mixed_ref[:, columns[h]] + total
+                for k in (1, 2, 3):
+                    z_copies[h, k].wait_recv()
+                    mixed_half = mixed_half + wide(z_in[h, k - 1])
+                if h == 0:
+                    left = mixed_half
+    right = mixed_half
+    total_sq = jnp.sum(left * left, axis=-1, keepdims=True) + jnp.sum(
+        right * right, axis=-1, keepdims=True
+    )
+    scale = lax.rsqrt(total_sq / width + 1e-06)
+    for h, value in enumerate((left, right)):
+        new_ref[:, columns[h]] = value.astype(jnp.bfloat16)
+        normed_ref[:, columns[h]] = (value * scale * gain_ref[:, columns[h]]).astype(jnp.bfloat16)
+    for copy in used:
+        copy.wait_send()
+
+
+BACK_COPIES = 2 * (16 + 8 + 4 + 3)
+
+
+def back(partial, mixed, final_gain):
+    rows, width = mixed.shape
+    half = width // 2
+    vmem = pl.BlockSpec(memory_space=pltpu.VMEM)
+    blocks = lambda *lead: pltpu.VMEM(lead + (rows, half), jnp.bfloat16)
+    return pl.pallas_call(
+        back_kernel,
+        out_shape=(jax.ShapeDtypeStruct((rows, width), jnp.bfloat16),) * 2,
+        in_specs=[vmem] * 3,
+        out_specs=(vmem, vmem),
+        scratch_shapes=[
+            blocks(2, 2, 4, 2),
+            blocks(2, 4, 2),
+            blocks(2, 4, 2),
+            blocks(2, 4),
+            blocks(2, 4),
+            blocks(2, 3),
+            blocks(2, 3),
+            pltpu.SemaphoreType.DMA((BACK_COPIES,)),
+            pltpu.SemaphoreType.DMA((BACK_COPIES,)),
+        ],
+        compiler_params=pltpu.CompilerParams(
+            collective_id=1, has_side_effects=True, vmem_limit_bytes=40 << 20
+        ),
+        name="back",
+    )(partial, mixed, final_gain.reshape(1, width))
 
 
 def migrate(kv_pages, page_pick, destination):
@@ -63,18 +339,37 @@
     rows, width = residual.shape
     local_experts = gate_up.shape[0]
     first = lax.axis_index("dp") * local_experts
-    arrived = migrate(kv_pages, page_pick, destination)
-    routes_all = lax.all_gather(routes, ("dp", "tensor"), axis=0, tiled=True)
+    grid = groups == 8 and shards == 4
+    if grid:
+        top_count = routes.shape[1]
+        extra = jnp.concatenate(
+            [routes, jnp.broadcast_to(destination, (rows, destination.shape[1]))], axis=1
+        ).astype(jnp.bfloat16)
+        extra = jnp.pad(extra, ((0, 0), (0, EXTRA - extra.shape[1])))
+        pages_all = lax.all_gather(kv_pages[page_pick[0]], "dp", axis=0)
+        mixed_sum, everything = front(attn_out, out_weight, residual, norm_gain, extra)
+        everything = everything.reshape(groups, shards * rows, width + EXTRA)
+        tokens = everything[:, :, :width].reshape(-1, width)
+        tail = everything[:, :, width:].astype(jnp.int32)
+        routes_all = tail[:, :, :top_count].reshape(-1, top_count)
+        owners = tail[:, 0, top_count : top_count + destination.shape[1]]
+        chosen = (owners == lax.axis_index("dp"))[:, :, None, None, None]
+        arrived = jnp.sum(jnp.where(chosen, pages_all, jnp.zeros((), kv_pages.dtype)), axis=0)
+    else:
+        arrived = migrate(kv_pages, page_pick, destination)
+        routes_all = lax.all_gather(routes, ("dp", "tensor"), axis=0, tiled=True)
+        projected = lax.psum_scatter(
+            jnp.dot(attn_out, out_weight, preferred_element_type=jnp.float32).astype(
+                jnp.bfloat16
+            ),
+            "tensor",
+            scatter_dimension=0,
+            tiled=True,
+        ).astype(jnp.float32)
+        mixed_sum = residual.astype(jnp.float32) + projected
+        normed_in = rms_scale(mixed_sum, norm_gain).astype(jnp.bfloat16)
+        tokens = lax.all_gather(normed_in, ("dp", "tensor"), axis=0, tiled=True)
     table = local_slots(routes_all, first, local_experts, groups, shards, rows)
-    projected = lax.psum_scatter(
-        jnp.dot(attn_out, out_weight, preferred_element_type=jnp.float32).astype(jnp.bfloat16),
-        "tensor",
-        scatter_dimension=0,
-        tiled=True,
-    ).astype(jnp.float32)
-    mixed_sum = residual.astype(jnp.float32) + projected
-    normed_in = rms_scale(mixed_sum, norm_gain).astype(jnp.bfloat16)
-    tokens = lax.all_gather(normed_in, ("dp", "tensor"), axis=0, tiled=True)
     local_router = lax.dynamic_slice_in_dim(router_weight, first, local_experts, axis=1)
     logits = jnp.dot(tokens, local_router, preferred_element_type=jnp.float32)
     gates = jax.nn.sigmoid(logits).astype(jnp.bfloat16)
@@ -99,6 +394,11 @@
     partial = jnp.einsum(
         "bts,bsd->btd", combine, expert_out, preferred_element_type=jnp.float32
     ).astype(jnp.bfloat16)
+    if grid:
+        new_residual, normed = back(
+            partial.reshape(4, 2, 2, 2, rows, width), mixed_sum, final_gain
+        )
+        return (new_residual, normed, arrived)
     moe_sum = lax.psum_scatter(
         partial.reshape(groups * shards * rows, width),
         ("dp", "tensor"),

time: 312 us -> 189 us (0.61)
  waiting for transfers between devices: 167 us -> 0 us
  Pallas kernels: 0 us -> 80.5 us
  blocking collectives: 62.8 us -> 33 us
  between operations: 13.9 us -> 0.83 us
  local copies, waits for them, and re-layouts: 13.4 us -> 25.1 us
  matrix products: 46.8 us -> 40.7 us
    reduce_scatter x2 -> x0, waiting for transfers between devices: 144 us -> none  [the longest x1 119 us: per_device(): lax.psum_scatter(partial.reshape(groups * shards * rows, width), ('dp', '...]
    pallas_call x0 -> x2, Pallas kernels: none -> 80.5 us  [the longest x1 41.2 us: front(): pl.pallas_call(front_kernel, out_shape=(jax.ShapeDtypeStruct((rows, width...]
    all_gather x1 -> x0, waiting for transfers between devices: 23.4 us -> none  [per_device(): tokens = lax.all_gather(normed_in, ('dp', 'tensor'), axis=0, tiled=True)]
    all_to_all x1 -> x0, blocking collectives: 21.3 us -> none  [migrate(): lax.all_to_all(outgoing, 'dp', split_axis=0, concat_axis=0, tiled=True)]
    unnamed x16 -> x20, local copies, waits for them, and re-layouts: 2.95 us -> 12.1 us
    all_gather x1, blocking collectives: 41.5 us -> 33 us  [per_device(): pages_all = lax.all_gather(kv_pages[page_pick[0]], 'dp', axis=0)]
    slice x0 -> x4, local copies, waits for them, and re-layouts: none -> 3.38 us  [the longest x1 2.93 us: per_device(): tokens = everything[:, :, :width].reshape(-1, width)]
  transfers between devices with their start and end apart: 3 -> 0, of which waited for: 3 -> 0; matrix products, arithmetic and copies ran while one was open for 1% -> 0% of each run, Pallas kernels for 0% -> 0%
where the time goes in v2:
time: 189 us; the launch traced here: 187 us
  Pallas kernels  80.5 us (43%)
  matrix products  40.7 us (22%)
  blocking collectives  33 us (17%)
  local copies, waits for them, and re-layouts  25.1 us (13%)
  other arithmetic  7.09 us (4%)
    pallas_call x1, Pallas kernels, front(): pl.pallas_call(front_kernel, out_shape=(jax.ShapeDtypeStruct((rows, width...  41.2 us
    pallas_call x1, Pallas kernels, back(): pl.pallas_call(back_kernel, out_shape=(jax.ShapeDtypeStruct((rows, width)...  39.3 us
    all_gather x1, blocking collectives, per_device(): pages_all = lax.all_gather(kv_pages[page_pick[0]], 'dp', axis=0)  33 us
    dot_general x1, matrix products, per_device(): jnp.einsum('becd,edgf->becgf', slotted, gate_up, preferred_element_type=j...  14.6 us
    unnamed x20, local copies, waits for them, and re-layouts  12.1 us
    dot_general x1, matrix products, per_device(): jnp.einsum('becf,efd->becd', hidden, down_weight, preferred_element_type=...  10.5 us
    convert_element_type x1, local copies, waits for them, and re-layouts, per_device(): expert_out = jnp.einsum('becf,efd->becd', hidden, down_weight, preferred_...  8.26 us
    dot_general x1, matrix products, per_device(): jnp.einsum('bts,btd->bsd', placement, tokens, preferred_element_type=jnp....  8.04 us

profile of v2, /device:TPU:0, one launch (start us, length us, event | category | flops | bytes accessed | tf_op | source)
XLA Modules:
  0.0 187.2 jit_solution(11191107609562145489)
XLA Ops:
  0.6 0.0 copy-start
  0.7 0.7 fusion.31
  1.4 0.7 convert_bitcast_fusion.1
  2.1 0.1 pad.6.clone
  2.1 0.7 convert.8
  2.8 0.1 pad_maximum_fusion
  2.9 0.1 eq.71
  3.0 0.1 copy.103
  3.1 0.0 copy-done
  3.1 0.6 gather_fusion
  3.8 33.0 %all-gather = bf16[16,16,4,256]{3,1,2,0:T(8,128)(2,1)S(1)} all-gather(bf16[2,16,4,256]{3,1,2,0:T(8,128)(2,1)S(1)} %copy.116), channel_id=2, replica_groups=mesh['dp'=8,'tensor'=4] {'dp'}, dimensions={0}, use_global_device_ids=true | all-gather | bytes 589824 | tf_op jit(solution)/shard_map/all_gather | solution.py:349
  36.8 0.0 copy-start.3
  36.8 1.6 copy-done.3
  38.4 0.0 copy-start.4
  38.4 0.9 copy-done.4
  39.3 0.0 copy-start.5
  39.3 0.9 copy-done.5
  40.2 0.7 copy-done.6
  40.9 41.2 %front.1 = (f32[40,2048]{1,0:T(8,128)S(1)}, bf16[4,2,2,2,40,2176]{5,4,3,2,1,0:T(8,128)(2,1)S(1)}) custom-call(bf16[160,512]{1,0:T(8,128)(2,1)S(1)} %copy-done.4, bf16[512,2048]{1,0:T(8,128)(2,1)S(1)} %copy-done.3, bf16[40,2048]{1,0:T(8,128)(2,1)S(1)} %copy-done.5, f32[1,2048]{1,0:T(1,128)S(1)} %bitcast.71, bf16[40,128]{1,0:T(8,128)(2,1)S(1)} %pad.4.extra_ref), custom_call_target="tpu_custom_call" | custom-call | tf_op jit(solution)/shard_map/front/pallas_call | solution.py:148
  82.1 0.0 copy-start.2
  82.1 2.5 %copy-done.2 = bf16[4,2,2,2,40,2176]{5,4,3,2,1,0:T(8,128)(2,1)} copy-done((bf16[4,2,2,2,40,2176]{5,4,3,2,1,0:T(8,128)(2,1)}, bf16[4,2,2,2,40,2176]{5,4,3,2,1,0:T(8,128)(2,1)S(1)}, u32[]{:S(2)}) %copy-start.2) | copy-done | bytes 5570584
  84.6 0.1 slice.26
  84.7 3.5 %copy.127 = bf16[8,160,128]{0,2,1:T(8,128)(2,1)} copy(bf16[8,160,128]{2,1,0:T(8,128)(2,1)S(1)} %slice.26) | data formatting | bytes 655360
  88.1 4.0 %convert_element_type.33 = s32[8,160,128]{0,2,1:T(8,128)S(1)} convert(bf16[8,160,128]{0,2,1:T(8,128)(2,1)} %copy.127) | non-fusion elementwise | flops 163840 | bytes 983040 | tf_op jit(solution)/shard_map/convert_element_type | solution.py:353
  92.1 0.1 slice.27
  92.2 0.3 copy.105
  92.5 0.1 eq.61
  92.6 0.1 compare_reduce_fusion
  92.8 0.1 copy.115
  92.8 0.1 select_reduce_fusion
  93.0 0.7 copy.117
  93.6 0.1 reshape.142
  93.7 0.2 fusion.20
  94.0 0.4 bitcast_compare_fusion
  94.4 2.9 %slice.28 = bf16[8,160,2048]{2,1,0:T(8,128)(2,1)S(1)} slice(bf16[8,160,2176]{2,1,0:T(8,128)(2,1)} %bitcast.69), slice={[0:8], [0:160], [0:2048]} | slice | bytes 10485760 | tf_op jit(solution)/shard_map/slice | solution.py:352
  97.3 2.2 %fusion.10 = bf16[1280,8]{0,1:T(8,128)(2,1)S(1)} fusion(bf16[1280,2048]{1,0:T(8,128)(2,1)S(1)} %bitcast.74, bf16[2048,64]{0,1:T(8,128)(2,1)} %param.16, s32[]{:T(128)S(6)} %select_n.54), kind=kOutput, calls=%fused_computation.13 | convolution fusion | flops 41984000 | bytes 5296132 | tf_op jit(solution)/shard_map/dot_general | solution.py:374
  99.5 0.1 reshape.144
  99.7 0.3 bitcast_select_fusion
  100.0 8.0 %convolution_convert_fusion = bf16[8,256,2048]{2,1,0:T(8,128)(2,1)} fusion(pred[8,160,256]{1,2,0:T(32,128)(4,1)S(1)} %bitcast_compare_fusion, bf16[8,160,2176]{2,1,0:T(8,128)(2,1)} %bitcast.70), kind=kOutput, calls=%fused_computation.7 | convolution fusion | flops 1346371584 | bytes 13959168 | tf_op jit(solution)/shard_map/bts,btd->bsd/dot_general | solution.py:382
  108.0 14.6 %fusion.11 = f32[8,8,32,2,256]{4,2,3,0,1:T(8,128)} fusion(bf16[8,2048,2,256,1]{3,2,1,0,4:T(2,128)(2,1)} %bitcast.77, bf16[8,8,32,2048,1]{3,2,1,0,4:T(8,128)(2,1)} %bitcast.75), kind=kOutput, calls=%fused_computation.14 | convolution fusion | flops 4294967296 | bytes 29360128 | tf_op jit(solution)/shard_map/becd,edgf->becgf/dot_general | solution.py:386
  122.7 10.5 %convert_bitcast_fusion = bf16[8,8,32,2048]{3,2,0,1:T(8,128)(2,1)} fusion(bf16[8,256,2048]{2,1,0:T(8,128)(2,1)} %param.19, f32[8,8,32,2,256]{4,2,3,0,1:T(8,128)} %fusion.11), kind=kOutput, calls=%fused_computation.6 | convolution fusion | flops 2154823680 | bytes 20971520 | tf_op jit(solution)/shard_map/becf,efd->becd/dot_general | solution.py:390
  133.2 8.3 %copy.113 = bf16[8,8,32,2048]{3,2,1,0:T(8,128)(2,1)} copy(bf16[8,8,32,2048]{3,2,0,1:T(8,128)(2,1)} %convert_bitcast_fusion) | data formatting | bytes 16777216 | tf_op jit(solution)/shard_map/convert_element_type | solution.py:392
  141.4 5.0 %convolution_convert_fusion.1 = bf16[8,160,2048]{2,1,0:T(8,128)(2,1)S(1)} fusion(bf16[8,160,256]{1,2,0:T(8,128)(2,1)S(1)} %bitcast_select_fusion, bf16[8,256,2048]{2,1,0:T(8,128)(2,1)} %bitcast.73), kind=kOutput, calls=%fused_computation.8 | convolution fusion | flops 1344798720 | bytes 14286848 | tf_op jit(solution)/shard_map/bts,bsd->btd/dot_general | solution.py:394
  146.5 0.0 copy-done.7
  146.5 39.3 %back.1 = (bf16[40,2048]{1,0:T(8,128)(2,1)S(1)}, bf16[40,2048]{1,0:T(8,128)(2,1)S(1)}) custom-call(bf16[4,2,2,2,40,2048]{5,4,3,2,1,0:T(8,128)(2,1)S(1)} %bitcast.67, f32[40,2048]{1,0:T(8,128)S(1)} %get-tuple-element.8.mixed_ref, f32[1,2048]{1,0:T(1,128)S(1)} %bitcast.72), custom_call_target="tpu_custom_call" | custom-call | tf_op jit(solution)/shard_map/back/pallas_call | solution.py:267
  185.8 0.7 copy.143
  186.5 0.7 copy.144
  187.2 0.0 copy-done.1
  (11 shorter events, 0.1 us)
Async XLA Ops:
  0.6 2.5 %copy-start = (bf16[32,16,4,256]{3,2,1,0:T(4,128)(2,1)S(1)}, bf16[32,16,4,256]{3,2,1,0:T(4,128)(2,1)}, u32[]{:S(2)}) copy-start(bf16[32,16,4,256]{3,2,1,0:T(4,128)(2,1)} %param.21) | copy-start | bytes 3145732
  36.8 1.6 copy-start.3
  38.4 0.9 copy-start.4
  39.3 0.9 copy-start.5
  40.2 0.7 copy-start.6
  82.1 2.5 %copy-start.2 = (bf16[4,2,2,2,40,2176]{5,4,3,2,1,0:T(8,128)(2,1)}, bf16[4,2,2,2,40,2176]{5,4,3,2,1,0:T(8,128)(2,1)S(1)}, u32[]{:S(2)}) copy-start(bf16[4,2,2,2,40,2176]{5,4,3,2,1,0:T(8,128)(2,1)S(1)} %get-tuple-element.7) | copy-start | bytes 16711684
  141.4 5.0 %copy-start.7 = (f32[2048]{0:T(1024)S(1)}, f32[2048]{0:T(1024)}, u32[]{:S(2)}) copy-start(f32[2048]{0:T(1024)} %param.20) | copy-start | bytes 24580
  141.4 45.7 %copy-start.1 = (bf16[32,16,4,256]{3,2,1,0:T(4,128)(2,1)S(1)}, bf16[32,16,4,256]{3,2,1,0:T(4,128)(2,1)}, u32[]{:S(2)}) copy-start(bf16[32,16,4,256]{3,2,1,0:T(4,128)(2,1)} %param.21) | copy-start | bytes 3145732

commit v3 on v2

--- a/solution.py
+++ b/solution.py
@@ -171,8 +171,8 @@
 
 
 def back_kernel(
-    partial_ref, mixed_ref, gain_ref, new_ref, normed_ref,
-    core_in, first_out, first_in, second_out, second_in, z_out, z_in, send_sems, recv_sems,
+    partial_ref, mixed_ref, gain_ref, pages_ref, chosen_ref, new_ref, normed_ref, arrived_ref,
+    pages_in, core_in, first_out, first_in, second_out, second_in, z_out, z_in, send_sems, recv_sems,
 ):
     at = Place()
     z, y, x, c = at.z, at.y, at.x, at.c
@@ -195,6 +195,9 @@
         return value.astype(jnp.float32)
 
     core_copies, first_copies, second_copies, z_copies = {}, {}, {}, {}
+    page_z = [
+        send(pages_ref, pages_in.at[j, 0], at.z_peers[j]) if j else None for j in range(4)
+    ]
     for first_other in (1, 0):
         for j in order:
             for h in (0, 1):
@@ -229,6 +232,12 @@
         for h in (0, 1):
             second_out[h, j] = gathered(h, j, 1).astype(jnp.bfloat16)
             second_copies[h, j] = send(second_out.at[h, j], second_in.at[h, j], second_peer[h])
+    page_y = []
+    for j in range(4):
+        if j:
+            page_z[j].wait_recv()
+        held = pages_in.at[j, 0] if j else pages_ref
+        page_y.append(send(held, pages_in.at[j, 1], at.y_peer))
     for j in order:
         for h in (0, 1):
             total = gathered(h, j, 0)
@@ -252,24 +261,35 @@
     for h, value in enumerate((left, right)):
         new_ref[:, columns[h]] = value.astype(jnp.bfloat16)
         normed_ref[:, columns[h]] = (value * scale * gain_ref[:, columns[h]]).astype(jnp.bfloat16)
+    for copy in page_y:
+        copy.wait_recv()
+    for slot in range(pages_ref.shape[0]):
+        found = jnp.zeros(pages_ref.shape[1:], jnp.float32)
+        for j in range(4):
+            for other in (0, 1):
+                held = pages_in[j, other, slot] if j or other else pages_ref[slot]
+                found = found + jnp.where(chosen_ref[slot, j, other] > 0, wide(held), 0.0)
+        arrived_ref[slot] = found.astype(jnp.bfloat16)
     for copy in used:
         copy.wait_send()
 
 
-BACK_COPIES = 2 * (16 + 8 + 4 + 3)
-
-
-def back(partial, mixed, final_gain):
+BACK_COPIES = 2 * (16 + 8 + 4 + 3) + 7
+
+
+def back(partial, mixed, final_gain, pages, chosen):
     rows, width = mixed.shape
     half = width // 2
     vmem = pl.BlockSpec(memory_space=pltpu.VMEM)
     blocks = lambda *lead: pltpu.VMEM(lead + (rows, half), jnp.bfloat16)
     return pl.pallas_call(
         back_kernel,
-        out_shape=(jax.ShapeDtypeStruct((rows, width), jnp.bfloat16),) * 2,
-        in_specs=[vmem] * 3,
-        out_specs=(vmem, vmem),
+        out_shape=(jax.ShapeDtypeStruct((rows, width), jnp.bfloat16),) * 2
+        + (jax.ShapeDtypeStruct(pages.shape, jnp.bfloat16),),
+        in_specs=[vmem] * 5,
+        out_specs=(vmem,) * 3,
         scratch_shapes=[
+            pltpu.VMEM((4, 2) + pages.shape, jnp.bfloat16),
             blocks(2, 2, 4, 2),
             blocks(2, 4, 2),
             blocks(2, 4, 2),
@@ -284,7 +304,108 @@
             collective_id=1, has_side_effects=True, vmem_limit_bytes=40 << 20
         ),
         name="back",
-    )(partial, mixed, final_gain.reshape(1, width))
+    )(partial, mixed, final_gain.reshape(1, width), pages, chosen)
+
+def dispatch_kernel(rows, top_count, all_ref, router_ref, named_ref, slots_ref, combine_ref):
+    width = router_ref.shape[0]
+    block = all_ref.shape[1]
+    span = router_ref.shape[1]
+    lanes = slots_ref.shape[2]
+    tokens = all_ref[0, :, :width]
+    tail = all_ref[0, :, width:].astype(jnp.float32)
+    named = named_ref[...]
+    hits = jnp.zeros((block, span), jnp.float32)
+    for k in range(top_count):
+        hits = hits + jnp.where(tail[:, k : k + 1] == named, 1.0, 0.0)
+    later = lax.broadcasted_iota(jnp.int32, (block, block), 0)
+    sooner = lax.broadcasted_iota(jnp.int32, (block, block), 1)
+    before = (later > sooner) & (later // rows == sooner // rows)
+    rank = jnp.dot(
+        jnp.where(before, 1.0, 0.0).astype(jnp.bfloat16),
+        hits.astype(jnp.bfloat16),
+        preferred_element_type=jnp.float32,
+    )
+    owner = lax.broadcasted_iota(jnp.int32, (block, span), 0) // rows
+    slot = lax.broadcasted_iota(jnp.int32, (block, span), 1) % lanes
+    wanted = (slot - owner * CAP).astype(jnp.float32)
+    table = jnp.where((hits > 0) & (rank == wanted), 1.0, 0.0)
+    logits = jnp.dot(tokens, router_ref[...], preferred_element_type=jnp.float32)
+    combine_ref[0] = (table * jax.nn.sigmoid(logits)).astype(jnp.bfloat16)
+    placed = lax.dot_general(
+        table.astype(jnp.bfloat16),
+        tokens,
+        (((0,), (0,)), ((), ())),
+        preferred_element_type=jnp.float32,
+    ).astype(jnp.bfloat16)
+    for e in range(slots_ref.shape[0]):
+        slots_ref[e, 0] = placed[e * lanes : (e + 1) * lanes]
+
+
+def dispatch(everything, router_slots, named, local_experts, rows, top_count):
+    groups, block, wide = everything.shape
+    width, span = router_slots.shape
+    lanes = span // local_experts
+    return pl.pallas_call(
+        lambda *refs: dispatch_kernel(rows, top_count, *refs),
+        grid=(groups,),
+        out_shape=(
+            jax.ShapeDtypeStruct((local_experts, groups, lanes, width), jnp.bfloat16),
+            jax.ShapeDtypeStruct((groups, block, span), jnp.bfloat16),
+        ),
+        in_specs=[
+            pl.BlockSpec((1, block, wide), lambda b: (b, 0, 0)),
+            pl.BlockSpec((width, span), lambda b: (0, 0)),
+            pl.BlockSpec((1, span), lambda b: (0, 0)),
+        ],
+        out_specs=(
+            pl.BlockSpec((local_experts, 1, lanes, width), lambda b: (0, b, 0, 0)),
+            pl.BlockSpec((1, block, span), lambda b: (b, 0, 0)),
+        ),
+        compiler_params=pltpu.CompilerParams(vmem_limit_bytes=40 << 20),
+        name="dispatch",
+    )(everything, router_slots, named)
+
+
+def finish_kernel(experts, groups, paired_ref, down_ref, combine_ref, out_ref, held):
+    step = pl.program_id(0)
+    lanes = held.shape[1] // experts
+
+    @pl.when(step < experts)
+    def _():
+        gate, up = paired_ref[0, 0], paired_ref[0, 1]
+        hidden = (gate / (1.0 + jnp.exp(-gate)) * up).astype(jnp.bfloat16)
+        made = jnp.dot(hidden, down_ref[0], preferred_element_type=jnp.float32)
+        spot = pl.ds(pl.multiple_of(step * lanes, lanes), lanes)
+        for b in range(groups):
+            held[b, spot, :] = made[b * lanes : (b + 1) * lanes].astype(jnp.bfloat16)
+
+    @pl.when(step >= experts)
+    def _():
+        out_ref[0] = jnp.dot(
+            combine_ref[0], held[step - experts], preferred_element_type=jnp.float32
+        ).astype(jnp.bfloat16)
+
+
+def finish(paired, down_weight, combine):
+    experts, _, slots, units = paired.shape
+    groups, block, span = combine.shape
+    width = down_weight.shape[2]
+    expert = lambda i: jnp.minimum(i, experts - 1)
+    group = lambda i: jnp.maximum(i - experts, 0)
+    return pl.pallas_call(
+        lambda *refs: finish_kernel(experts, groups, *refs),
+        grid=(experts + groups,),
+        out_shape=jax.ShapeDtypeStruct((groups, block, width), jnp.bfloat16),
+        in_specs=[
+            pl.BlockSpec((1, 2, slots, units), lambda i: (expert(i), 0, 0, 0)),
+            pl.BlockSpec((1, units, width), lambda i: (expert(i), 0, 0)),
+            pl.BlockSpec((1, block, span), lambda i: (group(i), 0, 0)),
+        ],
+        out_specs=pl.BlockSpec((1, block, width), lambda i: (group(i), 0, 0)),
+        scratch_shapes=[pltpu.VMEM((groups, span, width), jnp.bfloat16)],
+        compiler_params=pltpu.CompilerParams(vmem_limit_bytes=40 << 20),
+        name="finish",
+    )(paired, down_weight, combine)
 
 
 def migrate(kv_pages, page_pick, destination):
@@ -346,15 +467,40 @@
             [routes, jnp.broadcast_to(destination, (rows, destination.shape[1]))], axis=1
         ).astype(jnp.bfloat16)
         extra = jnp.pad(extra, ((0, 0), (0, EXTRA - extra.shape[1])))
-        pages_all = lax.all_gather(kv_pages[page_pick[0]], "dp", axis=0)
+        pages = kv_pages[page_pick[0]]
+        moved = pages.reshape(pages.shape[0], pages.shape[1], -1)
+        local_router = lax.dynamic_slice_in_dim(router_weight, first, local_experts, axis=1)
+        router_slots = jnp.repeat(local_router, shards * CAP, axis=1)
+        named = first + jnp.arange(local_experts * shards * CAP) // (shards * CAP)
         mixed_sum, everything = front(attn_out, out_weight, residual, norm_gain, extra)
+        owners = everything[:, 0, 0, 0, 0, width + top_count : width + top_count + 2]
+        owners_y = everything[:, 1, 0, 0, 0, width + top_count : width + top_count + 2]
+        owners = jnp.stack([owners, owners_y], axis=1).astype(jnp.int32)
+        chosen = owners == lax.axis_index("dp")
+        depth, side = lax.axis_index("dp") // 2, lax.axis_index("dp") % 2
+        chosen = chosen[(depth + 4 - jnp.arange(4)) % 4][:, (side + jnp.arange(2)) % 2]
+        chosen = chosen.transpose(2, 0, 1).astype(jnp.float32)
+        chosen = jnp.broadcast_to(chosen[..., None, None], chosen.shape + (1, moved.shape[2]))
         everything = everything.reshape(groups, shards * rows, width + EXTRA)
-        tokens = everything[:, :, :width].reshape(-1, width)
-        tail = everything[:, :, width:].astype(jnp.int32)
-        routes_all = tail[:, :, :top_count].reshape(-1, top_count)
-        owners = tail[:, 0, top_count : top_count + destination.shape[1]]
-        chosen = (owners == lax.axis_index("dp"))[:, :, None, None, None]
-        arrived = jnp.sum(jnp.where(chosen, pages_all, jnp.zeros((), kv_pages.dtype)), axis=0)
+        slotted, combine = dispatch(
+            everything,
+            router_slots,
+            named.astype(jnp.float32).reshape(1, -1),
+            local_experts,
+            rows,
+            top_count,
+        )
+        paired = jnp.einsum(
+            "emd,edgf->egmf",
+            slotted.reshape(local_experts, -1, width),
+            gate_up,
+            preferred_element_type=jnp.float32,
+        )
+        partial = finish(paired, down_weight, combine)
+        new_residual, normed, arrived = back(
+            partial.reshape(4, 2, 2, 2, rows, width), mixed_sum, final_gain, moved, chosen
+        )
+        return (new_residual, normed, arrived.reshape(pages.shape))
     else:
         arrived = migrate(kv_pages, page_pick, destination)
         routes_all = lax.all_gather(routes, ("dp", "tensor"), axis=0, tiled=True)
@@ -394,11 +540,6 @@
     partial = jnp.einsum(
         "bts,bsd->btd", combine, expert_out, preferred_element_type=jnp.float32
     ).astype(jnp.bfloat16)
-    if grid:
-        new_residual, normed = back(
-            partial.reshape(4, 2, 2, 2, rows, width), mixed_sum, final_gain
-        )
-        return (new_residual, normed, arrived)
     moe_sum = lax.psum_scatter(
         partial.reshape(groups * shards * rows, width),
         ("dp", "tensor"),

time: 189 us -> 145 us (0.77)
  blocking collectives: 33 us -> 0 us
  matrix products: 40.7 us -> 14.6 us
  Pallas kernels: 80.5 us -> 102 us
  other arithmetic: 7.09 us -> 1.59 us
    all_gather x1 -> x0, blocking collectives: 33 us -> none  [per_device(): pages_all = lax.all_gather(kv_pages[page_pick[0]], 'dp', axis=0)]
    dot_general x6 -> x1, matrix products: 40.7 us -> 14.6 us  [per_device(): jnp.einsum('emd,edgf->egmf', slotted.reshape(local_experts, -1, width), g...]
    pallas_call x0 -> x2, Pallas kernels: none -> 19.5 us  [the longest x1 10.4 us: finish(): pl.pallas_call(lambda *refs: finish_kernel(experts, groups, *refs), grid=...]
    convert_element_type x1, local copies, waits for them, and re-layouts: 8.26 us -> 0.11 us  [per_device(): chosen = chosen.transpose(2, 0, 1).astype(jnp.float32)]
    unnamed x20 -> x26, local copies, waits for them, and re-layouts: 12.1 us -> 17.4 us
    convert_element_type x1 -> x2, other arithmetic: 3.97 us -> 0.02 us  [the longest x1 0.01 us: per_device(): named.astype(jnp.float32).reshape(1, -1)]
    slice x4 -> x3, local copies, waits for them, and re-layouts: 3.38 us -> 0.29 us  [the longest x2 0.18 us: per_device(): owners = everything[:, 0, 0, 0, 0, width + top_count:width + top_count + 2]]
    pallas_call x1, Pallas kernels: 41.2 us -> 43.3 us  [front(): pl.pallas_call(front_kernel, out_shape=(jax.ShapeDtypeStruct((rows, width...]
where the time goes in v3:
time: 145 us; the launch traced here: 143 us
  Pallas kernels  102 us (70%)
  local copies, waits for them, and re-layouts  24.2 us (17%)
  matrix products  14.6 us (10%)
  other arithmetic  1.59 us (1%)
    pallas_call x1, Pallas kernels, front(): pl.pallas_call(front_kernel, out_shape=(jax.ShapeDtypeStruct((rows, width...  43.3 us
    pallas_call x1, Pallas kernels, back(): pl.pallas_call(back_kernel, out_shape=(jax.ShapeDtypeStruct((rows, width)...  39.4 us
    unnamed x26, local copies, waits for them, and re-layouts  17.4 us
    dot_general x1, matrix products, per_device(): jnp.einsum('emd,edgf->egmf', slotted.reshape(local_experts, -1, width), g...  14.6 us
    pallas_call x1, Pallas kernels, finish(): pl.pallas_call(lambda *refs: finish_kernel(experts, groups, *refs), grid=...  10.4 us
    pallas_call x1, Pallas kernels, dispatch(): pl.pallas_call(lambda *refs: dispatch_kernel(rows, top_count, *refs), gri...  9.11 us

profile of v3, /device:TPU:0, one launch (start us, length us, event | category | flops | bytes accessed | tf_op | source)
XLA Modules:
  0.0 143.4 jit_solution(1525129005851375561)
XLA Ops:
  0.6 0.0 copy-start
  0.7 0.8 convert.8
  1.5 0.7 convert_bitcast_fusion.1
  2.1 0.1 pad.8.clone
  2.2 0.1 pad_maximum_fusion
  2.3 0.1 copy.38
  2.4 0.0 copy-start.6
  2.4 1.6 %copy-done.6 = bf16[512,2048]{1,0:T(8,128)(2,1)S(1)} copy-done((bf16[512,2048]{1,0:T(8,128)(2,1)S(1)}, bf16[512,2048]{1,0:T(8,128)(2,1)}, u32[]{:S(2)}) %copy-start.6) | copy-done | bytes 2097176
  4.0 0.0 copy-start.7
  4.0 0.9 copy-done.7
  4.9 0.0 copy-start.8
  4.9 0.9 copy-done.8
  5.8 0.0 copy-start.9
  5.8 0.7 copy-done.9
  6.5 43.3 %front.1 = (f32[40,2048]{1,0:T(8,128)S(1)}, bf16[4,2,2,2,40,2176]{5,4,3,2,1,0:T(8,128)(2,1)S(1)}) custom-call(bf16[160,512]{1,0:T(8,128)(2,1)S(1)} %copy-done.7, bf16[512,2048]{1,0:T(8,128)(2,1)S(1)} %copy-done.6, bf16[40,2048]{1,0:T(8,128)(2,1)S(1)} %copy-done.8, f32[1,2048]{1,0:T(1,128)S(1)} %bitcast.29, bf16[40,128]{1,0:T(8,128)(2,1)S(1)} %pad.4.extra_ref), custom_call_target="tpu_custom_call" | custom-call | tf_op jit(solution)/shard_map/front/pallas_call | solution.py:148
  49.8 0.1 fusion.12
  49.9 0.0 copy-start.3
  49.9 2.4 %copy-done.3 = bf16[4,2,2,2,40,2176]{5,4,3,2,1,0:T(8,128)(2,1)} copy-done((bf16[4,2,2,2,40,2176]{5,4,3,2,1,0:T(8,128)(2,1)}, bf16[4,2,2,2,40,2176]{5,4,3,2,1,0:T(8,128)(2,1)S(1)}, u32[]{:S(2)}) %copy-start.3) | copy-done | bytes 5570584
  52.3 0.1 copy.41
  52.4 0.1 copy.43
  52.5 0.1 copy.42
  52.6 0.1 copy.44
  52.8 0.6 gather_fusion.1
  53.4 0.6 gather_fusion.2
  54.0 0.1 copy.46
  54.1 0.1 broadcast_in_dim.22.chosen_ref
  54.2 0.8 constant_dynamic-slice_fusion
  55.0 1.1 broadcast_in_dim.10
  56.1 1.5 %copy.39.refs_1_ = bf16[2048,256]{1,0:T(8,128)(2,1)S(1)} copy(bf16[2048,256]{0,1:T(8,128)(2,1)} %bitcast.31) | data formatting | bytes 2097152 | tf_op jit(solution)/shard_map/reshape | solution.py:473
  57.6 0.0 copy-start.4
  57.6 2.6 %copy-done.4 = bf16[4,2,2,2,40,2176]{5,4,3,2,1,0:T(8,128)(2,1)S(1)} copy-done((bf16[4,2,2,2,40,2176]{5,4,3,2,1,0:T(8,128)(2,1)S(1)}, bf16[4,2,2,2,40,2176]{5,4,3,2,1,0:T(8,128)(2,1)}, u32[]{:S(2)}) %copy-start.4) | copy-done | bytes 5570584
  60.2 9.1 %dispatch.1 = (bf16[8,8,32,2048]{3,2,1,0:T(8,128)(2,1)}, bf16[8,160,256]{2,1,0:T(8,128)(2,1)S(1)}) custom-call(bf16[8,160,2176]{2,1,0:T(8,128)(2,1)S(1)} %bitcast.28, bf16[2048,256]{1,0:T(8,128)(2,1)S(1)} %copy.39.refs_1_, f32[1,256]{1,0:T(1,128)S(1)} %fusion.6.refs_2_), custom_call_target="tpu_custom_call" | custom-call | tf_op jit(solution)/shard_map/dispatch/pallas_call | solution.py:348
  69.3 14.6 %fusion.2.refs_0_ = f32[8,2,256,256]{3,2,1,0:T(8,128)} fusion(bf16[8,256,2048,1]{2,1,3,0:T(8,128)(2,1)} %bitcast.34, bf16[8,2048,2,256]{3,2,1,0:T(2,128)(2,1)} %param.18), kind=kOutput, calls=%fused_computation.5 | convolution fusion | flops 4294967296 | bytes 29360128 | tf_op jit(solution)/shard_map/emd,edgf->egmf/dot_general | solution.py:493
  83.9 0.0 copy-start.5
  83.9 2.2 %copy-done.5 = f32[8,2,256,256]{3,2,1,0:T(8,128)S(1)} copy-done((f32[8,2,256,256]{3,2,1,0:T(8,128)S(1)}, f32[8,2,256,256]{3,2,1,0:T(8,128)}, u32[]{:S(2)}) %copy-start.5) | copy-done | bytes 4194328
  86.1 10.4 %finish.1 = bf16[8,160,2048]{2,1,0:T(8,128)(2,1)S(1)} custom-call(f32[8,2,256,256]{3,2,1,0:T(8,128)S(1)} %copy-done.5, bf16[8,256,2048]{2,1,0:T(8,128)(2,1)} %refs_1_.1, bf16[8,160,256]{2,1,0:T(8,128)(2,1)S(1)} %get-tuple-element.12.refs_2_), custom_call_target="tpu_custom_call" | custom-call | tf_op jit(solution)/shard_map/finish/pallas_call | solution.py:395
  96.5 0.0 copy-start.1
  96.5 2.3 %copy-done.1 = bf16[8,160,2048]{2,1,0:T(8,128)(2,1)} copy-done((bf16[8,160,2048]{2,1,0:T(8,128)(2,1)}, bf16[8,160,2048]{2,1,0:T(8,128)(2,1)S(1)}, u32[]{:S(2)}) %copy-start.1) | copy-done | bytes 5242904
  98.8 0.0 copy-done.11
  98.8 0.0 copy-done
  98.9 0.6 gather_fusion
  99.5 0.0 copy-done.10
  99.5 0.0 copy-start.2
  99.5 2.5 %copy-done.2 = bf16[8,160,2048]{2,1,0:T(8,128)(2,1)S(1)} copy-done((bf16[8,160,2048]{2,1,0:T(8,128)(2,1)S(1)}, bf16[8,160,2048]{2,1,0:T(8,128)(2,1)}, u32[]{:S(2)}) %copy-start.2) | copy-done | bytes 5242904
  102.0 39.4 %back.1 = (bf16[40,2048]{1,0:T(8,128)(2,1)S(1)}, bf16[40,2048]{1,0:T(8,128)(2,1)S(1)}, bf16[2,16,1024]{2,1,0:T(8,128)(2,1)S(1)}) custom-call(bf16[4,2,2,2,40,2048]{5,4,3,2,1,0:T(8,128)(2,1)S(1)} %bitcast.27, f32[40,2048]{1,0:T(8,128)S(1)} %get-tuple-element.13.mixed_ref, f32[1,2048]{1,0:T(1,128)S(1)} %bitcast.30, ...), custom_call_target="tpu_custom_call" | custom-call | tf_op jit(solution)/shard_map/back/pallas_call | solution.py:285
  141.4 0.7 reshape.207
  142.1 0.7 copy.54
  142.8 0.7 copy.55
  (14 shorter events, 0.1 us)
Async XLA Ops:
  0.6 98.2 %copy-start = (bf16[32,16,4,256]{3,2,1,0:T(4,128)(2,1)S(1)}, bf16[32,16,4,256]{3,2,1,0:T(4,128)(2,1)}, u32[]{:S(2)}) copy-start(bf16[32,16,4,256]{3,2,1,0:T(4,128)(2,1)} %param.21) | copy-start | bytes 3145732
  2.4 1.6 %copy-start.6 = (bf16[512,2048]{1,0:T(8,128)(2,1)S(1)}, bf16[512,2048]{1,0:T(8,128)(2,1)}, u32[]{:S(2)}) copy-start(bf16[512,2048]{1,0:T(8,128)(2,1)} %weight_ref.1) | copy-start | bytes 6291460
  4.0 0.9 copy-start.7
  4.9 0.9 copy-start.8
  5.8 0.7 copy-start.9
  49.9 2.4 %copy-start.3 = (bf16[4,2,2,2,40,2176]{5,4,3,2,1,0:T(8,128)(2,1)}, bf16[4,2,2,2,40,2176]{5,4,3,2,1,0:T(8,128)(2,1)S(1)}, u32[]{:S(2)}) copy-start(bf16[4,2,2,2,40,2176]{5,4,3,2,1,0:T(8,128)(2,1)S(1)} %get-tuple-element.10) | copy-start | bytes 16711684
  57.6 2.6 %copy-start.4 = (bf16[4,2,2,2,40,2176]{5,4,3,2,1,0:T(8,128)(2,1)S(1)}, bf16[4,2,2,2,40,2176]{5,4,3,2,1,0:T(8,128)(2,1)}, u32[]{:S(2)}) copy-start(bf16[4,2,2,2,40,2176]{5,4,3,2,1,0:T(8,128)(2,1)} %copy-done.3) | copy-start | bytes 16711684
  83.9 2.2 %copy-start.5 = (f32[8,2,256,256]{3,2,1,0:T(8,128)S(1)}, f32[8,2,256,256]{3,2,1,0:T(8,128)}, u32[]{:S(2)}) copy-start(f32[8,2,256,256]{3,2,1,0:T(8,128)} %fusion.2.refs_0_) | copy-start | bytes 12582916
  86.1 12.8 %copy-start.11 = (s32[1,2]{1,0:T(1,128)S(1)}, s32[1,2]{1,0:T(1,128)}, u32[]{:S(2)}) copy-start(s32[1,2]{1,0:T(1,128)} %param.22) | copy-start | bytes 28
  86.1 13.4 %copy-start.10 = (f32[2048]{0:T(1024)S(1)}, f32[2048]{0:T(1024)}, u32[]{:S(2)}) copy-start(f32[2048]{0:T(1024)} %param.20) | copy-start | bytes 24580
  96.5 2.3 %copy-start.1 = (bf16[8,160,2048]{2,1,0:T(8,128)(2,1)}, bf16[8,160,2048]{2,1,0:T(8,128)(2,1)S(1)}, u32[]{:S(2)}) copy-start(bf16[8,160,2048]{2,1,0:T(8,128)(2,1)S(1)} %finish.1) | copy-start | bytes 15728644
  99.5 2.5 %copy-start.2 = (bf16[8,160,2048]{2,1,0:T(8,128)(2,1)S(1)}, bf16[8,160,2048]{2,1,0:T(8,128)(2,1)}, u32[]{:S(2)}) copy-start(bf16[8,160,2048]{2,1,0:T(8,128)(2,1)} %copy-done.1) | copy-start | bytes 15728644

commit v4 on v3

--- a/solution.py
+++ b/solution.py
@@ -164,7 +164,7 @@
             pltpu.SemaphoreType.DMA((FRONT_COPIES,)),
         ],
         compiler_params=pltpu.CompilerParams(
-            collective_id=0, has_side_effects=True, vmem_limit_bytes=40 << 20
+            collective_id=0, has_side_effects=True, vmem_limit_bytes=12 << 20
         ),
         name="front",
     )(attn_out, out_weight, residual, norm_gain.reshape(1, width), extra)
@@ -196,8 +196,9 @@
 
     core_copies, first_copies, second_copies, z_copies = {}, {}, {}, {}
     page_z = [
-        send(pages_ref, pages_in.at[j, 0], at.z_peers[j]) if j else None for j in range(4)
+        send(pages_ref, pages_in.at[z, y], at.z_peers[j]) if j else None for j in range(4)
     ]
+    pages_in[z, y] = pages_ref[...]
     for first_other in (1, 0):
         for j in order:
             for h in (0, 1):
@@ -236,8 +237,8 @@
     for j in range(4):
         if j:
             page_z[j].wait_recv()
-        held = pages_in.at[j, 0] if j else pages_ref
-        page_y.append(send(held, pages_in.at[j, 1], at.y_peer))
+        spot = pages_in.at[(z + 4 - j) % 4, y]
+        page_y.append(send(spot if j else pages_ref, spot, at.y_peer))
     for j in order:
         for h in (0, 1):
             total = gathered(h, j, 0)
@@ -265,10 +266,10 @@
         copy.wait_recv()
     for slot in range(pages_ref.shape[0]):
         found = jnp.zeros(pages_ref.shape[1:], jnp.float32)
-        for j in range(4):
-            for other in (0, 1):
-                held = pages_in[j, other, slot] if j or other else pages_ref[slot]
-                found = found + jnp.where(chosen_ref[slot, j, other] > 0, wide(held), 0.0)
+        for zs in range(4):
+            for ys in (0, 1):
+                held = wide(pages_in[zs, ys, slot])
+                found = found + jnp.where(chosen_ref[zs, ys, slot] > 0, held, 0.0)
         arrived_ref[slot] = found.astype(jnp.bfloat16)
     for copy in used:
         copy.wait_send()
@@ -301,7 +302,7 @@
             pltpu.SemaphoreType.DMA((BACK_COPIES,)),
         ],
         compiler_params=pltpu.CompilerParams(
-            collective_id=1, has_side_effects=True, vmem_limit_bytes=40 << 20
+            collective_id=1, has_side_effects=True, vmem_limit_bytes=20 << 20
         ),
         name="back",
     )(partial, mixed, final_gain.reshape(1, width), pages, chosen)
@@ -361,7 +362,7 @@
             pl.BlockSpec((local_experts, 1, lanes, width), lambda b: (0, b, 0, 0)),
             pl.BlockSpec((1, block, span), lambda b: (b, 0, 0)),
         ),
-        compiler_params=pltpu.CompilerParams(vmem_limit_bytes=40 << 20),
+        compiler_params=pltpu.CompilerParams(vmem_limit_bytes=50 << 20),
         name="dispatch",
     )(everything, router_slots, named)
 
@@ -403,7 +404,7 @@
         ],
         out_specs=pl.BlockSpec((1, block, width), lambda i: (group(i), 0, 0)),
         scratch_shapes=[pltpu.VMEM((groups, span, width), jnp.bfloat16)],
-        compiler_params=pltpu.CompilerParams(vmem_limit_bytes=40 << 20),
+        compiler_params=pltpu.CompilerParams(vmem_limit_bytes=24 << 20),
         name="finish",
     )(paired, down_weight, combine)
 
@@ -473,13 +474,8 @@
         router_slots = jnp.repeat(local_router, shards * CAP, axis=1)
         named = first + jnp.arange(local_experts * shards * CAP) // (shards * CAP)
         mixed_sum, everything = front(attn_out, out_weight, residual, norm_gain, extra)
-        owners = everything[:, 0, 0, 0, 0, width + top_count : width + top_count + 2]
-        owners_y = everything[:, 1, 0, 0, 0, width + top_count : width + top_count + 2]
-        owners = jnp.stack([owners, owners_y], axis=1).astype(jnp.int32)
-        chosen = owners == lax.axis_index("dp")
-        depth, side = lax.axis_index("dp") // 2, lax.axis_index("dp") % 2
-        chosen = chosen[(depth + 4 - jnp.arange(4)) % 4][:, (side + jnp.arange(2)) % 2]
-        chosen = chosen.transpose(2, 0, 1).astype(jnp.float32)
+        owners = everything[:, :, 0, 0, 0, width + top_count : width + top_count + 2]
+        chosen = (owners.astype(jnp.int32) == lax.axis_index("dp")).astype(jnp.float32)
         chosen = jnp.broadcast_to(chosen[..., None, None], chosen.shape + (1, moved.shape[2]))
         everything = everything.reshape(groups, shards * rows, width + EXTRA)
         slotted, combine = dispatch(

time: 145 us -> 137 us (0.945)
  local copies, waits for them, and re-layouts: 24.2 us -> 16.3 us
    unnamed x26 -> x20, local copies, waits for them, and re-layouts: 17.4 us -> 13.3 us
    pallas_call x1, Pallas kernels: 10.4 us -> 6.57 us  [finish(): pl.pallas_call(lambda *refs: finish_kernel(experts, groups, *refs), grid=...]
    pallas_call x1, Pallas kernels: 9.11 us -> 11.7 us  [dispatch(): pl.pallas_call(lambda *refs: dispatch_kernel(rows, top_count, *refs), gri...]
where the time goes in v4:
time: 137 us; the launch traced here: 135 us
  Pallas kernels  101 us (74%)
  local copies, waits for them, and re-layouts  16.3 us (12%)
  matrix products  14.6 us (11%)
  other arithmetic  2.27 us (2%)
    pallas_call x1, Pallas kernels, front(): pl.pallas_call(front_kernel, out_shape=(jax.ShapeDtypeStruct((rows, width...  43.3 us
    pallas_call x1, Pallas kernels, back(): pl.pallas_call(back_kernel, out_shape=(jax.ShapeDtypeStruct((rows, width)...  39.5 us
    dot_general x1, matrix products, per_device(): jnp.einsum('emd,edgf->egmf', slotted.reshape(local_experts, -1, width), g...  14.6 us
    unnamed x20, local copies, waits for them, and re-layouts  13.3 us
    pallas_call x1, Pallas kernels, dispatch(): pl.pallas_call(lambda *refs: dispatch_kernel(rows, top_count, *refs), gri...  11.7 us
    pallas_call x1, Pallas kernels, finish(): pl.pallas_call(lambda *refs: finish_kernel(experts, groups, *refs), grid=...  6.57 us

profile of v4, /device:TPU:0, one launch (start us, length us, event | category | flops | bytes accessed | tf_op | source)
XLA Modules:
  0.0 134.9 jit_solution(135777373965482571)
XLA Ops:
  0.6 0.0 copy-start
  0.7 0.7 fusion.7
  1.4 0.7 convert_bitcast_fusion
  2.1 0.1 pad.6.clone
  2.1 0.7 convert.8
  2.8 0.1 pad_maximum_fusion
  2.9 0.1 copy.30
  3.0 0.8 constant_dynamic-slice_fusion
  3.8 0.0 copy-done
  3.8 0.6 gather_fusion
  4.4 0.1 broadcast_in_dim.19
  4.6 0.5 copy.31.refs_1_
  5.1 0.0 copy-start.4
  5.1 1.6 %copy-done.4 = bf16[512,2048]{1,0:T(8,128)(2,1)S(1)} copy-done((bf16[512,2048]{1,0:T(8,128)(2,1)S(1)}, bf16[512,2048]{1,0:T(8,128)(2,1)}, u32[]{:S(2)}) %copy-start.4) | copy-done | bytes 2097176
  6.7 0.0 copy-start.5
  6.7 0.9 copy-done.5
  7.6 0.0 copy-start.6
  7.6 0.9 copy-done.6
  8.5 0.0 copy-start.7
  8.5 0.7 copy-done.7
  9.2 43.3 %front.1 = (f32[40,2048]{1,0:T(8,128)S(1)}, bf16[4,2,2,2,40,2176]{5,4,3,2,1,0:T(8,128)(2,1)S(1)}) custom-call(bf16[160,512]{1,0:T(8,128)(2,1)S(1)} %copy-done.5, bf16[512,2048]{1,0:T(8,128)(2,1)S(1)} %copy-done.4, bf16[40,2048]{1,0:T(8,128)(2,1)S(1)} %copy-done.6, f32[1,2048]{1,0:T(1,128)S(1)} %bitcast.22, bf16[40,128]{1,0:T(8,128)(2,1)S(1)} %pad.4.extra_ref), custom_call_target="tpu_custom_call" | custom-call | tf_op jit(solution)/shard_map/front/pallas_call | solution.py:148
  52.5 0.0 copy-start.2
  52.5 0.1 compare_convert_fusion
  52.6 0.1 broadcast_in_dim.20.chosen_ref
  52.7 2.3 %copy-done.2 = bf16[4,2,2,2,40,2176]{5,4,3,2,1,0:T(8,128)(2,1)} copy-done((bf16[4,2,2,2,40,2176]{5,4,3,2,1,0:T(8,128)(2,1)}, bf16[4,2,2,2,40,2176]{5,4,3,2,1,0:T(8,128)(2,1)S(1)}, u32[]{:S(2)}) %copy-start.2) | copy-done | bytes 5570584
  55.0 11.7 %dispatch.1 = (bf16[8,8,32,2048]{3,2,1,0:T(8,128)(2,1)}, bf16[8,160,256]{2,1,0:T(8,128)(2,1)S(1)}) custom-call(bf16[8,160,2176]{2,1,0:T(8,128)(2,1)} %bitcast.21, bf16[2048,256]{1,0:T(8,128)(2,1)S(1)} %copy.31.refs_1_, f32[1,256]{1,0:T(1,128)S(1)} %fusion.6.refs_2_), custom_call_target="tpu_custom_call" | custom-call | tf_op jit(solution)/shard_map/dispatch/pallas_call | solution.py:349
  66.7 14.6 %fusion.2.refs_0_ = f32[8,2,256,256]{3,2,1,0:T(8,128)} fusion(bf16[8,256,2048,1]{2,1,3,0:T(8,128)(2,1)} %bitcast.26, bf16[8,2048,2,256]{3,2,1,0:T(2,128)(2,1)} %param.18), kind=kOutput, calls=%fused_computation.3 | convolution fusion | flops 4294967296 | bytes 29360128 | tf_op jit(solution)/shard_map/emd,edgf->egmf/dot_general | solution.py:489
  81.3 0.0 copy-start.1
  81.3 3.4 %copy-done.1 = bf16[8,256,2048]{2,1,0:T(8,128)(2,1)S(1)} copy-done((bf16[8,256,2048]{2,1,0:T(8,128)(2,1)S(1)}, bf16[8,256,2048]{2,1,0:T(8,128)(2,1)}, u32[]{:S(2)}) %copy-start.1) | copy-done | bytes 8388632
  84.7 0.0 copy-start.3
  84.7 2.2 %copy-done.3 = f32[8,2,256,256]{3,2,1,0:T(8,128)S(1)} copy-done((f32[8,2,256,256]{3,2,1,0:T(8,128)S(1)}, f32[8,2,256,256]{3,2,1,0:T(8,128)}, u32[]{:S(2)}) %copy-start.3) | copy-done | bytes 4194328
  86.9 0.0 copy-start.8
  86.9 6.6 %finish.1 = bf16[8,160,2048]{2,1,0:T(8,128)(2,1)S(1)} custom-call(f32[8,2,256,256]{3,2,1,0:T(8,128)S(1)} %copy-done.3, bf16[8,256,2048]{2,1,0:T(8,128)(2,1)S(1)} %copy-done.1, bf16[8,160,256]{2,1,0:T(8,128)(2,1)S(1)} %get-tuple-element.12.refs_2_), custom_call_target="tpu_custom_call" | custom-call | tf_op jit(solution)/shard_map/finish/pallas_call | solution.py:396
  93.5 0.0 copy-done.8
  93.5 39.5 %back.1 = (bf16[40,2048]{1,0:T(8,128)(2,1)S(1)}, bf16[40,2048]{1,0:T(8,128)(2,1)S(1)}, bf16[2,16,1024]{2,1,0:T(8,128)(2,1)S(1)}) custom-call(bf16[4,2,2,2,40,2048]{5,4,3,2,1,0:T(8,128)(2,1)S(1)} %bitcast.20, f32[40,2048]{1,0:T(8,128)S(1)} %get-tuple-element.13.mixed_ref, f32[1,2048]{1,0:T(1,128)S(1)} %bitcast.23, ...), custom_call_target="tpu_custom_call" | custom-call | tf_op jit(solution)/shard_map/back/pallas_call | solution.py:286
  133.0 0.7 reshape.120
  133.6 0.7 copy.43
  134.3 0.7 copy.44
  (4 shorter events, 0.1 us)
Async XLA Ops:
  0.6 3.2 %copy-start = (bf16[32,16,4,256]{3,2,1,0:T(4,128)(2,1)S(1)}, bf16[32,16,4,256]{3,2,1,0:T(4,128)(2,1)}, u32[]{:S(2)}) copy-start(bf16[32,16,4,256]{3,2,1,0:T(4,128)(2,1)} %param.21) | copy-start | bytes 3145732
  5.1 1.6 %copy-start.4 = (bf16[512,2048]{1,0:T(8,128)(2,1)S(1)}, bf16[512,2048]{1,0:T(8,128)(2,1)}, u32[]{:S(2)}) copy-start(bf16[512,2048]{1,0:T(8,128)(2,1)} %weight_ref.1) | copy-start | bytes 6291460
  6.7 0.9 copy-start.5
  7.6 0.9 copy-start.6
  8.5 0.7 copy-start.7
  52.5 2.5 %copy-start.2 = (bf16[4,2,2,2,40,2176]{5,4,3,2,1,0:T(8,128)(2,1)}, bf16[4,2,2,2,40,2176]{5,4,3,2,1,0:T(8,128)(2,1)S(1)}, u32[]{:S(2)}) copy-start(bf16[4,2,2,2,40,2176]{5,4,3,2,1,0:T(8,128)(2,1)S(1)} %get-tuple-element.10) | copy-start | bytes 16711684
  81.3 3.4 %copy-start.1 = (bf16[8,256,2048]{2,1,0:T(8,128)(2,1)S(1)}, bf16[8,256,2048]{2,1,0:T(8,128)(2,1)}, u32[]{:S(2)}) copy-start(bf16[8,256,2048]{2,1,0:T(8,128)(2,1)} %refs_1_.1) | copy-start | bytes 25165828
  84.7 2.2 %copy-start.3 = (f32[8,2,256,256]{3,2,1,0:T(8,128)S(1)}, f32[8,2,256,256]{3,2,1,0:T(8,128)}, u32[]{:S(2)}) copy-start(f32[8,2,256,256]{3,2,1,0:T(8,128)} %fusion.2.refs_0_) | copy-start | bytes 12582916
  86.9 6.6 %copy-start.8 = (f32[2048]{0:T(1024)S(1)}, f32[2048]{0:T(1024)}, u32[]{:S(2)}) copy-start(f32[2048]{0:T(1024)} %param.20) | copy-start | bytes 24580
